TPU v7x, 128 devices: a whole 4x4x4 slice. The times are simulated.
128 devices in a mesh: slab: 4 (over y), energy: 32 (over z, x, core).
Axes of the slice: x: 4, y: 4, z: 4, core: 2. Of those that a mesh axis runs over, the one named last changes fastest.
Arguments:
- link_p: float32 [12, 2, 64, 64], P('slab'), may hold values from -1 to 2, as said below
- link_q: float32 [12, 2, 64, 64], P('slab'), may hold values from -1 to 2, as said below
- shift: float32 [64, 12, 64], P('energy', 'slab'), may hold values from 0.01 to 0.3
- lesser_gain: float32 [64, 12, 64], P('energy', 'slab'), may hold values from 0.1 to 2
- sources: float32 [12, 2, 64, 128], P('slab'), may hold values from -1.8 to 1.8
Outputs:
- polar: float32 [2, 64, 12, 64, 128], P(None, None, 'slab', 'energy')
Inputs may be any that keep to these rules, and one draw needn't show every extreme that they name: `link_p`: real and imaginary parts of complex link factors. `link_q`: real and imaginary parts of complex link factors.
All inputs are finite; a program needn't handle non-finite values.
Results may differ from a plain program's by a relative error of at most 0.0003.
Values sent between devices are 32-bit elements; how exact they have to be, the bound alone decides.
A program may use at most 64 MiB of HBM per device.

v0:
```python
import math

import jax
import jax.numpy as jnp
from jax import lax
from jax.sharding import PartitionSpec as P

HIGHEST = lax.Precision.HIGHEST


def real_form(part):
    real = part[..., 0, :, :]
    imag = part[..., 1, :, :]
    upper_half = jnp.concatenate([real, -imag], axis=-1)
    lower_half = jnp.concatenate([imag, real], axis=-1)
    return jnp.concatenate([upper_half, lower_half], axis=-2)


def from_half(half):
    orbits = half.shape[-1]
    return real_form(jnp.stack([half[..., :orbits, :], half[..., orbits:, :]], axis=-3))


def right_transposed(left, right):
    return jnp.einsum("...ij,...kj->...ik", left, right, precision=HIGHEST)


def left_transposed(left, right):
    return jnp.einsum("...ji,...jk->...ik", left, right, precision=HIGHEST)


def product(left, right):
    return jnp.einsum("...ij,...jk->...ik", left, right, precision=HIGHEST)


def solve_with(factor, rhs):
    return jax.scipy.linalg.cho_solve((factor, True), rhs)


def forward_retarded(diag, upper, rhs):
    width = diag.shape[-1]
    opening = jnp.broadcast_to(jnp.swapaxes(upper[0], 0, 1), diag[1].shape)
    start = (diag[1], opening, rhs[1], diag[0], rhs[0])

    def sweep(carry, pieces):
        current, coupling, carried_rhs, corner, port_rhs = carry
        link_block, diag_after, rhs_after = pieces
        factor = jnp.linalg.cholesky(current)
        stacked = jnp.concatenate(
            [jnp.broadcast_to(link_block, current.shape), coupling, carried_rhs], axis=-1
        )
        solved = solve_with(factor, stacked)
        step_link = solved[..., :width]
        step_port = solved[..., width : 2 * width]
        step_rhs = solved[..., 2 * width :]
        corner = corner - left_transposed(coupling, step_port)
        port_rhs = port_rhs - left_transposed(coupling, step_rhs)
        current = diag_after - left_transposed(link_block, step_link)
        coupling = -left_transposed(link_block, step_port)
        carried_rhs = rhs_after - left_transposed(link_block, step_rhs)
        return (
            (current, coupling, carried_rhs, corner, port_rhs),
            (factor, step_link, step_port, step_rhs),
        )

    return lax.scan(sweep, start, (upper[1:], diag[2:], rhs[2:]))


def forward_lesser(factors, step_link, step_port, rhs):

    def sweep(carry, pieces):
        carried_rhs, port_rhs = carry
        factor, link_step, port_step, rhs_after = pieces
        step_rhs = solve_with(factor, carried_rhs)
        port_rhs = port_rhs - left_transposed(port_step, carried_rhs)
        carried_rhs = rhs_after - left_transposed(link_step, carried_rhs)
        return ((carried_rhs, port_rhs), step_rhs)

    final, steps = lax.scan(sweep, (rhs[1], rhs[0]), (factors, step_link, step_port, rhs[2:]))
    return (final[1], final[0], steps)


def back_substitute(step_link, step_port, step_rhs, first_port, last_port):

    def climb(carry, pieces):
        link_step, port_step, rhs_step = pieces
        value = rhs_step - product(link_step, carry) - product(port_step, first_port)
        return (value, value)

    unused, inner_rows = lax.scan(climb, last_port, (step_link, step_port, step_rhs), reverse=True)
    return jnp.concatenate([first_port[None], inner_rows, last_port[None]], axis=0)


def chain_factor(blocks, uppers):
    factors = []
    steps = []
    current = blocks[0]
    for position in range(len(blocks)):
        factor = jnp.linalg.cholesky(current)
        factors.append(factor)
        if position + 1 < len(blocks):
            step = solve_with(factor, uppers[position])
            steps.append(step)
            current = blocks[position + 1] - left_transposed(uppers[position], step)
    return (factors, steps)


def chain_solve(factors, steps, uppers, rhs_list):
    partial_rows = []
    carried = rhs_list[0]
    for position in range(len(factors)):
        solved = solve_with(factors[position], carried)
        partial_rows.append(solved)
        if position + 1 < len(factors):
            carried = rhs_list[position + 1] - left_transposed(uppers[position], solved)
    values = [partial_rows[-1]]
    for position in range(len(factors) - 2, -1, -1):
        values.insert(0, partial_rows[position] - product(steps[position], values[0]))
    return jnp.stack(values, axis=0)


def correlate(lesser_re, lesser_im, power):
    count = power.shape[1]
    length = 2 * count
    freqs = jnp.arange(length, dtype=jnp.int32)
    moments = jnp.arange(count, dtype=jnp.int32)
    phase = (freqs[:, None] * moments[None, :] % length).astype(jnp.float32) * (
        2.0 * math.pi / length
    )
    cos_table = jnp.cos(phase)
    sin_table = jnp.sin(phase)

    def transform(table, values):
        return jnp.einsum("kt,itor->kior", table, values, precision=HIGHEST)

    def inverse(table, values):
        return jnp.einsum("wk,kior->wior", table, values, precision=HIGHEST)

    spec_re = transform(cos_table, lesser_re) + transform(sin_table, lesser_im)
    spec_im = transform(cos_table, lesser_im) - transform(sin_table, lesser_re)
    power_cos = transform(cos_table, power)
    power_sin = transform(sin_table, power)
    mixed_re = spec_re * power_cos - spec_im * power_sin
    mixed_im = spec_re * power_sin + spec_im * power_cos
    scale = 1.0 / (length * count)
    back_cos = jnp.swapaxes(cos_table, 0, 1) * scale
    back_sin = jnp.swapaxes(sin_table, 0, 1) * scale
    corr_re = inverse(back_cos, mixed_re) - inverse(back_sin, mixed_im)
    corr_im = inverse(back_sin, mixed_re) + inverse(back_cos, mixed_im)
    return jnp.stack([corr_re, corr_im], axis=0)


def per_device(link_p, link_q, shift, lesser_gain, sources):
    slabs = link_p.shape[0]
    orbits = link_p.shape[2]
    width = 2 * orbits
    columns = sources.shape[-1]
    energies = shift.shape[0]
    owner = lax.axis_index("slab")
    devices = lax.axis_size("slab")
    rp = real_form(link_p)
    rq = real_form(link_q)
    pp = right_transposed(rp, rp)
    qq = right_transposed(rq, rq)
    cc = -right_transposed(rp, rq)
    lead = jnp.where(owner == 0, 1.0, 0.0).astype(jnp.float32)
    inner_sum = qq[:-1] + pp[1:]
    base = jnp.concatenate([(inner_sum[0] + lead * pp[0])[None], inner_sum[1:], qq[-1:]], axis=0)
    upper = cc[1:]
    eye = jnp.eye(width, dtype=jnp.float32)
    shift_slab = jnp.swapaxes(jnp.concatenate([shift, shift], axis=-1), 0, 1)
    diag = base[:, None] + eye * shift_slab[..., None, :]
    sources_flat = sources.reshape(slabs, width, columns)
    rhs = jnp.broadcast_to(sources_flat[:, None], (slabs, energies, width, columns))
    final, stored = forward_retarded(diag, upper, rhs)
    last_diag, coupling, last_rhs, corner, port_rhs = final
    factors, step_link, step_port, step_rhs = stored
    first_half = corner[..., :orbits]
    link_half = jnp.swapaxes(coupling, -1, -2)[..., :orbits]
    last_half = last_diag[..., :orbits]
    gathered = (
        lax.all_gather(first_half[None], "slab", axis=0, tiled=True),
        lax.all_gather(link_half[None], "slab", axis=0, tiled=True),
        lax.all_gather(last_half[None], "slab", axis=0, tiled=True),
        lax.all_gather(port_rhs[None], "slab", axis=0, tiled=True),
        lax.all_gather(last_rhs[None], "slab", axis=0, tiled=True),
        lax.all_gather(cc[0][..., :orbits][None], "slab", axis=0, tiled=True),
        lax.all_gather(pp[0][..., :orbits][None], "slab", axis=0, tiled=True),
    )
    heads, links, tails, head_rhs, tail_rhs, left_links, left_terms = gathered
    blocks = []
    uppers = []
    rhs_list = []
    for member in range(devices):
        blocks.append(from_half(heads[member]))
        tail_block = from_half(tails[member])
        rhs_list.append(head_rhs[member])
        rhs_list.append(tail_rhs[member])
        uppers.append(from_half(links[member]))
        if member + 1 < devices:
            tail_block = tail_block + from_half(left_terms[member + 1])
            uppers.append(jnp.broadcast_to(from_half(left_links[member + 1]), tail_block.shape))
        blocks.append(tail_block)
    chain_factors, chain_steps = chain_factor(blocks, uppers)
    ports = chain_solve(chain_factors, chain_steps, uppers, rhs_list)
    first_port = lax.dynamic_index_in_dim(ports, 2 * owner, 0, keepdims=False)
    last_port = lax.dynamic_index_in_dim(ports, 2 * owner + 1, 0, keepdims=False)
    retarded = back_substitute(step_link, step_port, step_rhs, first_port, last_port)
    gain_slab = jnp.swapaxes(jnp.concatenate([lesser_gain, lesser_gain], axis=-1), 0, 1)
    lesser_rhs = gain_slab[..., None] * retarded
    head_lesser, tail_lesser, lesser_steps = forward_lesser(
        factors, step_link, step_port, lesser_rhs
    )
    lesser_heads, lesser_tails = (
        lax.all_gather(head_lesser[None], "slab", axis=0, tiled=True),
        lax.all_gather(tail_lesser[None], "slab", axis=0, tiled=True),
    )
    lesser_list = []
    for member in range(devices):
        lesser_list.append(lesser_heads[member])
        lesser_list.append(lesser_tails[member])
    lesser_ports = chain_solve(chain_factors, chain_steps, uppers, lesser_list)
    first_lesser = lax.dynamic_index_in_dim(lesser_ports, 2 * owner, 0, keepdims=False)
    last_lesser = lax.dynamic_index_in_dim(lesser_ports, 2 * owner + 1, 0, keepdims=False)
    lesser = back_substitute(step_link, step_port, lesser_steps, first_lesser, last_lesser)
    ret_real = retarded[:, :, :orbits]
    ret_imag = retarded[:, :, orbits:]
    les_real = lesser[:, :, :orbits]
    les_imag = lesser[:, :, orbits:]
    elem_re = ret_real * les_real + ret_imag * les_imag
    elem_im = ret_real * les_imag - ret_imag * les_real
    elem_power = ret_real * ret_real + ret_imag * ret_imag
    return correlate(
        lax.all_to_all(elem_re, "energy", split_axis=2, concat_axis=1, tiled=True),
        lax.all_to_all(elem_im, "energy", split_axis=2, concat_axis=1, tiled=True),
        lax.all_to_all(elem_power, "energy", split_axis=2, concat_axis=1, tiled=True),
    )


def solution(mesh):
    placed = (
        P("slab", None, None, None),
        P("slab", None, None, None),
        P("energy", "slab", None),
        P("energy", "slab", None),
        P("slab", None, None, None),
    )
    return jax.shard_map(
        per_device,
        mesh=mesh,
        in_specs=placed,
        out_specs=P(None, None, "slab", "energy", None),
        check_vma=False,
    )
```

profile of v0, /device:TPU:1, one launch (start us, length us, event | category | flops | bytes accessed | tf_op | source)
XLA Modules:
  0.0 622.6 jit_solution(18332154761071906548)
XLA Ops:
  5.0 23.5 %custom-call.48 = f32[2,128,128]{2,1,0:T(8,128)S(1)} custom-call(f32[2,128,128]{2,1,0:T(8,128)S(1)} %fusion.19), custom_call_target="Cholesky" | custom-call | tf_op jit(solution)/shard_map/while/body/eval_jaxpr/jit(cholesky)/cholesky | solution.py:48
  28.8 19.7 %custom-call.16 = f32[2,1,128,128]{2,3,1,0:T(8,128)S(1)} custom-call(f32[2,1,128,128]{3,2,1,0:T(8,128)S(1)} %fusion.129), custom_call_target="InvertDiagBlocksLowerTriangular" | custom-call | tf_op jit(solution)/shard_map/while/body/eval_jaxpr/jit(_cho_solve)/vmap()/triangular_solve | solution.py:37
  52.2 11.2 %all-gather.3 = f32[8,128,64]{1,2,0:T(8,128)S(1)} all-gather(f32[2,128,64]{1,2,0:T(8,128)S(1)} %slice_subtract_fusion), channel_id=5, replica_groups=mesh['slab'=4,'energy'=32] {'slab'}, dimensions={0}, use_global_device_ids=true | all-gather | bytes 327680 | tf_op jit(solution)/shard_map/all_gather | solution.py:184
  64.2 9.6 %all-gather = f32[8,128,64]{1,2,0:T(8,128)S(1)} all-gather(f32[2,128,64]{1,2,0:T(8,128)S(1)} %slice_subtract_fusion.1), channel_id=2, replica_groups=mesh['slab'=4,'energy'=32] {'slab'}, dimensions={0}, use_global_device_ids=true | all-gather | bytes 327680 | tf_op jit(solution)/shard_map/all_gather | solution.py:182
  74.3 23.5 %custom-call.49 = f32[2,128,128]{2,1,0:T(8,128)S(1)} custom-call(f32[2,128,128]{2,1,0:T(8,128)S(1)} %fusion.121), custom_call_target="Cholesky" | custom-call | tf_op jit(solution)/shard_map/jit(cholesky)/cholesky | solution.py:99
  98.0 19.7 %custom-call.50 = f32[2,1,128,128]{2,3,1,0:T(8,128)S(1)} custom-call(f32[2,1,128,128]{3,2,1,0:T(8,128)S(1)} %select_bitcast_fusion.7), custom_call_target="InvertDiagBlocksLowerTriangular" | custom-call | tf_op jit(solution)/shard_map/jit(_cho_solve)/vmap()/triangular_solve | solution.py:37
  117.7 9.4 %all-gather.2 = f32[8,128,64]{1,2,0:T(8,128)S(1)} all-gather(f32[2,128,64]{1,2,0:T(8,128)S(1)} %slice_negate_fusion), channel_id=4, replica_groups=mesh['slab'=4,'energy'=32] {'slab'}, dimensions={0}, use_global_device_ids=true | all-gather | bytes 327680 | tf_op jit(solution)/shard_map/all_gather | solution.py:183
  128.1 10.4 %all-gather.4 = f32[512,64]{1,0:T(8,128)S(1)} all-gather(f32[128,64]{1,0:T(8,128)S(1)} %bitcast.537), channel_id=6, replica_groups=mesh['slab'=4,'energy'=32] {'slab'}, dimensions={0}, use_global_device_ids=true | all-gather | bytes 163840 | tf_op jit(solution)/shard_map/all_gather | solution.py:188
  140.0 23.5 %custom-call.52 = f32[2,128,128]{2,1,0:T(8,128)S(1)} custom-call(f32[2,128,128]{2,1,0:T(8,128)S(1)} %fusion.110), custom_call_target="Cholesky" | custom-call | tf_op jit(solution)/shard_map/jit(cholesky)/cholesky | solution.py:99
  163.8 19.7 %custom-call.53 = f32[2,1,128,128]{2,3,1,0:T(8,128)S(1)} custom-call(f32[2,1,128,128]{3,2,1,0:T(8,128)S(1)} %select_bitcast_fusion.6), custom_call_target="InvertDiagBlocksLowerTriangular" | custom-call | tf_op jit(solution)/shard_map/jit(_cho_solve)/vmap()/triangular_solve | solution.py:37
  183.5 9.1 %all-gather.6 = f32[512,64]{0,1:T(8,128)S(1)} all-gather(f32[128,64]{0,1:T(8,128)S(1)} %slice.581), channel_id=8, replica_groups=mesh['slab'=4,'energy'=32] {'slab'}, dimensions={0}, use_global_device_ids=true | all-gather | bytes 163840 | tf_op jit(solution)/shard_map/all_gather | solution.py:187
  194.8 23.6 %custom-call.55 = f32[2,128,128]{2,1,0:T(8,128)S(1)} custom-call(f32[2,128,128]{2,1,0:T(8,128)S(1)} %fusion.97), custom_call_target="Cholesky" | custom-call | tf_op jit(solution)/shard_map/jit(cholesky)/cholesky | solution.py:99
  218.7 19.7 %custom-call.56 = f32[2,1,128,128]{2,3,1,0:T(8,128)S(1)} custom-call(f32[2,1,128,128]{3,2,1,0:T(8,128)S(1)} %select_bitcast_fusion.5), custom_call_target="InvertDiagBlocksLowerTriangular" | custom-call | tf_op jit(solution)/shard_map/jit(_cho_solve)/vmap()/triangular_solve | solution.py:37
  240.2 23.5 %custom-call.58 = f32[2,128,128]{2,1,0:T(8,128)S(1)} custom-call(f32[2,128,128]{2,1,0:T(8,128)S(1)} %fusion.84), custom_call_target="Cholesky" | custom-call | tf_op jit(solution)/shard_map/jit(cholesky)/cholesky | solution.py:99
  263.9 19.9 %custom-call.59 = f32[2,1,128,128]{2,3,1,0:T(8,128)S(1)} custom-call(f32[2,1,128,128]{3,2,1,0:T(8,128)S(1)} %select_bitcast_fusion.4), custom_call_target="InvertDiagBlocksLowerTriangular" | custom-call | tf_op jit(solution)/shard_map/jit(_cho_solve)/vmap()/triangular_solve | solution.py:37
  285.9 23.5 %custom-call.61 = f32[2,128,128]{2,1,0:T(8,128)S(1)} custom-call(f32[2,128,128]{2,1,0:T(8,128)S(1)} %fusion.71), custom_call_target="Cholesky" | custom-call | tf_op jit(solution)/shard_map/jit(cholesky)/cholesky | solution.py:99
  309.6 19.7 %custom-call.62 = f32[2,1,128,128]{2,3,1,0:T(8,128)S(1)} custom-call(f32[2,1,128,128]{3,2,1,0:T(8,128)S(1)} %select_bitcast_fusion.3), custom_call_target="InvertDiagBlocksLowerTriangular" | custom-call | tf_op jit(solution)/shard_map/jit(_cho_solve)/vmap()/triangular_solve | solution.py:37
  332.3 23.9 %custom-call.64 = f32[2,128,128]{2,1,0:T(8,128)S(1)} custom-call(f32[2,128,128]{2,1,0:T(8,128)S(1)} %fusion.58), custom_call_target="Cholesky" | custom-call | tf_op jit(solution)/shard_map/jit(cholesky)/cholesky | solution.py:99
  356.4 19.7 %custom-call.65 = f32[2,1,128,128]{2,3,1,0:T(8,128)S(1)} custom-call(f32[2,1,128,128]{3,2,1,0:T(8,128)S(1)} %select_bitcast_fusion.2), custom_call_target="InvertDiagBlocksLowerTriangular" | custom-call | tf_op jit(solution)/shard_map/jit(_cho_solve)/vmap()/triangular_solve | solution.py:37
  378.2 23.5 %custom-call.67 = f32[2,128,128]{2,1,0:T(8,128)S(1)} custom-call(f32[2,128,128]{2,1,0:T(8,128)S(1)} %fusion.45), custom_call_target="Cholesky" | custom-call | tf_op jit(solution)/shard_map/jit(cholesky)/cholesky | solution.py:99
  401.9 19.8 %custom-call.68 = f32[2,1,128,128]{2,3,1,0:T(8,128)S(1)} custom-call(f32[2,1,128,128]{3,2,1,0:T(8,128)S(1)} %select_bitcast_fusion.1), custom_call_target="InvertDiagBlocksLowerTriangular" | custom-call | tf_op jit(solution)/shard_map/jit(_cho_solve)/vmap()/triangular_solve | solution.py:37
  423.9 23.5 %custom-call.70 = f32[2,128,128]{2,1,0:T(8,128)S(1)} custom-call(f32[2,128,128]{2,1,0:T(8,128)S(1)} %fusion.32), custom_call_target="Cholesky" | custom-call | tf_op jit(solution)/shard_map/jit(cholesky)/cholesky | solution.py:99
  447.6 19.7 %custom-call.71 = f32[2,1,128,128]{2,3,1,0:T(8,128)S(1)} custom-call(f32[2,1,128,128]{3,2,1,0:T(8,128)S(1)} %select_bitcast_fusion), custom_call_target="InvertDiagBlocksLowerTriangular" | custom-call | tf_op jit(solution)/shard_map/jit(_cho_solve)/vmap()/triangular_solve | solution.py:37
  467.7 9.9 %all-gather.1 = f32[8,128,128]{2,1,0:T(8,128)S(1)} all-gather(f32[2,128,128]{2,1,0:T(8,128)S(1)} %convolution_subtract_fusion.43), channel_id=3, replica_groups=mesh['slab'=4,'energy'=32] {'slab'}, dimensions={0}, use_global_device_ids=true | all-gather | bytes 655360 | tf_op jit(solution)/shard_map/all_gather | solution.py:185
  484.0 10.5 %all-gather.5 = f32[8,128,128]{2,1,0:T(8,128)S(1)} all-gather(f32[2,128,128]{2,1,0:T(8,128)} %copy.167), channel_id=7, replica_groups=mesh['slab'=4,'energy'=32] {'slab'}, dimensions={0}, use_global_device_ids=true | all-gather | bytes 655360 | tf_op jit(solution)/shard_map/all_gather | solution.py:186
  515.9 9.9 %all-gather.8 = f32[8,128,128]{2,1,0:T(8,128)S(1)} all-gather(f32[2,128,128]{2,1,0:T(8,128)S(1)} %convolution_subtract_fusion.18), channel_id=10, replica_groups=mesh['slab'=4,'energy'=32] {'slab'}, dimensions={0}, use_global_device_ids=true | all-gather | bytes 655360 | tf_op jit(solution)/shard_map/all_gather | solution.py:216
  525.8 10.1 %all-gather.7 = f32[8,128,128]{2,1,0:T(8,128)S(1)} all-gather(f32[2,128,128]{2,1,0:T(8,128)S(1)} %convolution_subtract_fusion.19), channel_id=9, replica_groups=mesh['slab'=4,'energy'=32] {'slab'}, dimensions={0}, use_global_device_ids=true | all-gather | bytes 655360 | tf_op jit(solution)/shard_map/all_gather | solution.py:215
  550.7 33.5 %all-to-all-start.2 = ((f32[3,2,64,128]{3,1,0,2:T(2,128)}), f32[3,2,64,128]{3,1,0,2:T(2,128)S(1)}, u32[]{:S(2)}, u32[]{:S(2)}) async-start(f32[3,2,64,128]{3,1,0,2:T(2,128)} %copy.247), calls=%async_computation.2 | async-start | bytes 393216 | tf_op jit(solution)/shard_map/all_to_all | solution.py:236
  585.8 6.6 %all-to-all-done.2 = f32[3,2,64,128]{3,1,0,2:T(2,128)S(1)} async-done(((f32[3,2,64,128]{3,1,0,2:T(2,128)}), f32[3,2,64,128]{3,1,0,2:T(2,128)S(1)}, u32[]{:S(2)}, u32[]{:S(2)}) %all-to-all-start.2) | async-done | bytes 196640 | tf_op jit(solution)/shard_map/all_to_all | solution.py:236
  597.6 6.9 %all-to-all-done = f32[3,2,64,128]{3,1,0,2:T(2,128)S(1)} async-done(((f32[3,2,64,128]{3,1,0,2:T(2,128)}), f32[3,2,64,128]{3,1,0,2:T(2,128)S(1)}, u32[]{:S(2)}, u32[]{:S(2)}) %all-to-all-start) | async-done | bytes 196640 | tf_op jit(solution)/shard_map/all_to_all | solution.py:234
  604.5 4.2 all-to-all-start.1
  609.4 7.4 %all-to-all-done.1 = f32[3,2,64,128]{3,1,0,2:T(2,128)S(1)} async-done(((f32[3,2,64,128]{3,1,0,2:T(2,128)}), f32[3,2,64,128]{3,1,0,2:T(2,128)S(1)}, u32[]{:S(2)}, u32[]{:S(2)}) %all-to-all-start.1) | async-done | bytes 196640 | tf_op jit(solution)/shard_map/all_to_all | solution.py:235
  (330 shorter events, 82.4 us)
Async XLA Ops:
  0.0 1.1 copy-start.29
  0.0 1.2 copy-start.30
  3.1 0.8 slice-start
  48.4 1.0 copy-start.34
  127.3 12.1 %copy-start.2 = (f32[2,64,64]{2,1,0:T(8,128)}, f32[2,64,64]{2,1,0:T(8,128)S(1)}, u32[]{:S(2)}) copy-start(f32[2,64,64]{2,1,0:T(8,128)S(1)} %neg.73) | copy-start | bytes 98308
  127.4 12.1 %copy-start.4 = (f32[2,64,64]{2,1,0:T(8,128)}, f32[2,64,64]{2,1,0:T(8,128)S(1)}, u32[]{:S(2)}) copy-start(f32[2,64,64]{2,1,0:T(8,128)S(1)} %copy.316) | copy-start | bytes 98308
  163.7 19.8 %copy-start.35 = (f32[128,128]{0,1:T(8,128)S(1)}, f32[128,128]{0,1:T(8,128)}, u32[]{:S(2)}) copy-start(f32[128,128]{0,1:T(8,128)} %get-tuple-element.164) | copy-start | bytes 196612
  238.5 1.1 copy-start.9
  238.6 1.0 copy-start.12
  329.4 2.3 copy-start.18
  329.5 2.3 copy-start.21
  422.4 0.8 copy-start.31
  422.4 0.9 copy-start.32
  447.5 19.8 %copy-start.33 = (f32[1,2,64,128]{3,2,1,0:T(8,128)S(1)}, f32[1,2,64,128]{3,2,1,0:T(8,128)}, u32[]{:S(2)}) copy-start(f32[1,2,64,128]{3,2,1,0:T(8,128)} %get-tuple-element.171) | copy-start | bytes 196612
  483.9 10.5 %copy-start.3 = (f32[2,64,64]{2,1,0:T(8,128)S(1)}, f32[2,64,64]{2,1,0:T(8,128)}, u32[]{:S(2)}) copy-start(f32[2,64,64]{2,1,0:T(8,128)} %copy-done.2) | copy-start | bytes 98308
  484.0 10.5 %copy-start.5 = (f32[2,64,64]{2,1,0:T(8,128)S(1)}, f32[2,64,64]{2,1,0:T(8,128)}, u32[]{:S(2)}) copy-start(f32[2,64,64]{2,1,0:T(8,128)} %copy-done.4) | copy-start | bytes 98308
  484.0 10.5 %copy-start.27 = (f32[2,128,128]{2,1,0:T(8,128)S(1)}, f32[2,128,128]{2,1,0:T(8,128)}, u32[]{:S(2)}) copy-start(f32[2,128,128]{2,1,0:T(8,128)} %fusion.118) | copy-start | bytes 393220
  495.3 0.8 copy-start.7
  496.8 0.8 copy-start.10
  496.8 0.9 copy-start.13
  498.5 0.8 copy-start.16
  500.1 0.8 copy-start.19
  500.1 0.9 copy-start.22
  501.8 0.8 copy-start.25
  503.3 0.8 copy-start.1
  537.4 0.8 copy-start.8
  538.9 0.9 copy-start.14
  542.2 0.9 copy-start.23
  543.9 0.8 copy-start.26
  550.7 41.7 %all-to-all-start.2 = ((f32[3,2,64,128]{3,1,0,2:T(2,128)}), f32[3,2,64,128]{3,1,0,2:T(2,128)S(1)}, u32[]{:S(2)}, u32[]{:S(2)}) async-start(f32[3,2,64,128]{3,1,0,2:T(2,128)} %copy.247), calls=%async_computation.2 | async-start | bytes 393216 | tf_op jit(solution)/shard_map/all_to_all | solution.py:236
  592.4 12.1 %all-to-all-start = ((f32[3,2,64,128]{3,1,0,2:T(2,128)}), f32[3,2,64,128]{3,1,0,2:T(2,128)S(1)}, u32[]{:S(2)}, u32[]{:S(2)}) async-start(f32[3,2,64,128]{3,1,0,2:T(2,128)} %copy.243), calls=%async_computation | async-start | bytes 393216 | tf_op jit(solution)/shard_map/all_to_all | solution.py:234
  604.5 12.4 %all-to-all-start.1 = ((f32[3,2,64,128]{3,1,0,2:T(2,128)}), f32[3,2,64,128]{3,1,0,2:T(2,128)S(1)}, u32[]{:S(2)}, u32[]{:S(2)}) async-start(f32[3,2,64,128]{3,1,0,2:T(2,128)} %copy.245), calls=%async_computation.1 | async-start | bytes 393216 | tf_op jit(solution)/shard_map/all_to_all | solution.py:235
  (14 other events, 10.4 us)
where the time goes:
time: 631 us; the launch traced here: 623 us
  other arithmetic  394 us (62%)
  blocking collectives  90.1 us (14%)
  matrix products  43 us (7%)
  starting transfers between devices  41.5 us (7%)
  local copies, waits for them, and re-layouts  30.7 us (5%)
  waiting for transfers between devices  20.9 us (3%)
    another operation x25, other arithmetic, chain_factor(): factor = jnp.linalg.cholesky(current)  189 us
    another operation x19, other arithmetic, solve_with(): return jax.scipy.linalg.cho_solve((factor, True), rhs)  178 us
    all_to_all x1, starting transfers between devices, per_device(): lax.all_to_all(elem_power, 'energy', split_axis=2, concat_axis=1, tiled=T...  33.5 us
    another operation x3, other arithmetic, sweep(): factor = jnp.linalg.cholesky(current)  23.6 us
    another operation x50, matrix products, solve_with(): return jax.scipy.linalg.cho_solve((factor, True), rhs)  17.6 us
    unnamed x110, local copies, waits for them, and re-layouts  16 us
  transfers between devices with their start and end apart: 3, of which 3 were waited for; matrix products, arithmetic and copies ran while one was open for 1% of the time, Pallas kernels for 0%

commit v1 on v0

v1 whole, which is shorter than its diff:
```python
import functools

import jax
import jax.numpy as jnp
from jax import lax
from jax.experimental import pallas as pl
from jax.experimental.pallas import tpu as pltpu
from jax.sharding import PartitionSpec as P

HIGHEST = lax.Precision.HIGHEST
F32 = jnp.float32
ORB = 64
LANES = 128
SLABS = 12
LEVELS = (
    ((0, None, 1), (2, 1, 3), (4, 3, 5), (6, 5, 7), (8, 7, 9), (10, 9, 11)),
    ((1, None, 3), (5, 3, 7), (9, 7, 11)),
    ((3, None, 7), (11, 7, None)),
    ((7, None, None),),
)
STEPS = {6: 1, 3: 2, 2: 2, 1: 4}


def lane_of(shape):
    return lax.broadcasted_iota(jnp.int32, shape, len(shape) - 1)


def row_of(shape):
    return lax.broadcasted_iota(jnp.int32, shape, len(shape) - 2)


def times_i(value):
    turned = pltpu.roll(value, ORB, 1)
    return jnp.where(lane_of(value.shape) < ORB, -turned, turned)


def right_form(value):
    return jnp.concatenate([value, times_i(value)], axis=0)


def dot(left, right):
    return jnp.dot(left, right, precision=HIGHEST, preferred_element_type=F32)


def pivot_inverse(diag, cross, size):
    if size == 1:
        return [[(1.0 / diag[0], None)]]
    if size == 2:
        re, im = cross[0, 1]
        scale = 1.0 / (diag[0] * diag[1] - re * re - im * im)
        re, im = re * scale, im * scale
        return [[(diag[1] * scale, None), (-re, -im)], [(-re, im), (diag[0] * scale, None)]]
    held = {(i, i): (diag[i], None) for i in range(size)}
    held.update(cross)

    def entry(i, j):
        if i <= j:
            return held[i, j]
        return (held[j, i][0], -held[j, i][1])

    for p in range(size):
        inverse = 1.0 / held[p, p][0]
        row = {j: entry(p, j) for j in range(size) if j != p}
        scaled = {j: (row[j][0] * inverse, row[j][1] * inverse) for j in row}
        after = {(p, p): (-inverse, None)}
        for i in row:
            for j in row:
                if i > j:
                    continue
                real = held[i, j][0] - row[i][0] * scaled[j][0] - row[i][1] * scaled[j][1]
                imag = None
                if i != j:
                    imag = held[i, j][1] - row[i][0] * scaled[j][1] + row[i][1] * scaled[j][0]
                after[i, j] = (real, imag)
        for j in row:
            if p < j:
                after[p, j] = scaled[j]
            else:
                after[j, p] = (scaled[j][0], -scaled[j][1])
        held = after
    out = []
    for i in range(size):
        out.append([])
        for j in range(size):
            real, imag = entry(i, j) if i != j else held[i, i]
            out[i].append((-real, None if imag is None else -imag))
    return out


def invert_all(values, size):
    lanes = lane_of((1, LANES))
    rows = row_of((ORB, LANES))
    zero = jnp.zeros((1, LANES), F32)
    for k in range(0, ORB, size):
        later = []
        for value in values:
            tops = [value[k + j : k + j + 1, :] for j in range(size)]
            turned = [times_i(top) for top in tops]
            cols = []
            for j in range(size):
                at = k + j
                cols.append(
                    (
                        jnp.broadcast_to(value[:, at : at + 1], (ORB, LANES)),
                        jnp.broadcast_to(value[:, ORB + at : ORB + at + 1], (ORB, LANES)),
                    )
                )
            diag = [cols[j][0][k + j : k + j + 1] for j in range(size)]
            cross = {}
            for i in range(size):
                for j in range(i + 1, size):
                    cross[i, j] = (cols[j][0][k + i : k + i + 1], cols[j][1][k + i : k + i + 1])
            small = pivot_inverse(diag, cross, size)
            fresh = []
            for i in range(size):
                plain = zero
                rotated = zero
                for j in range(size):
                    real, imag = small[i][j]
                    plain = plain + real * tops[j]
                    rotated = rotated + real * turned[j]
                    if imag is not None:
                        plain = plain + imag * turned[j]
                        rotated = rotated - imag * tops[j]
                for j in range(size):
                    real, imag = small[i][j]
                    imag = zero if imag is None else imag
                    on_real, on_imag = lanes == k + j, lanes == ORB + k + j
                    plain = jnp.where(on_real, real, jnp.where(on_imag, imag, plain))
                    rotated = jnp.where(on_real, -imag, jnp.where(on_imag, real, rotated))
                fresh.append((plain, rotated))
            inside = lanes & (ORB - 1)
            inside = (inside >= k) & (inside < k + size)
            total = jnp.where(inside, 0.0, value)
            for j in range(size):
                total = total - cols[j][0] * fresh[j][0] - cols[j][1] * fresh[j][1]
            for j in range(size):
                total = jnp.where(rows == k + j, fresh[j][0], total)
            later.append(total)
        values = later
    return values


def solve_kernel(p_ref, q_ref, src_ref, shift_ref, gain_ref, out_ref, diag, link, inv, rhs, sol):
    slot = {}

    def at(i, j):
        return slot.setdefault((i, j), len(slot))

    corner = lane_of((ORB, LANES)) == row_of((ORB, LANES))
    for s in range(SLABS):
        p, q = p_ref[s], q_ref[s]
        left = jnp.concatenate([p, q], axis=0)
        right = jnp.concatenate([p, times_i(p), q, times_i(q)], axis=0)
        both = lax.dot_general(
            left, right, (((1,), (1,)), ((), ())), precision=HIGHEST, preferred_element_type=F32
        )
        own = both[ORB:, LANES:]
        before = both[:ORB, :LANES]
        shift = jnp.broadcast_to(shift_ref[s : s + 1, :], (ORB, LANES))
        own = own + jnp.where(corner, shift, 0.0)
        if s == 0:
            diag[s] = own + before
        else:
            diag[s] = own
            diag[s - 1] = diag[s - 1] + before
            link[at(s - 1, s)] = -both[:ORB, LANES:]
            link[at(s, s - 1)] = -both[ORB:, :LANES]
        rhs[s] = src_ref[s]

    plan = []
    for level in LEVELS:
        inverses = invert_all([diag[s] for s, _, _ in level], STEPS[len(level)])
        for (s, l, r), inverse in zip(level, inverses):
            inv[s] = inverse
        updates = []
        for s, l, r in level:
            near = [n for n in (l, r) if n is not None]
            sides = [right_form(link[at(s, n)]) for n in near] + [right_form(rhs[s])]
            step = dot(inv[s], jnp.concatenate(sides, axis=1))
            rhs[s] = step[:, LANES * len(near) :]
            if not near:
                continue
            back = jnp.concatenate([link[at(n, s)] for n in near], axis=0)
            pieces = [step[:, LANES * i : LANES * (i + 1)] for i in range(len(near) + 1)]
            moved = dot(back, jnp.concatenate([right_form(piece) for piece in pieces], axis=1))
            for i, n in enumerate(near):
                link[at(s, n)] = pieces[i]
                for j, m in enumerate(near):
                    block = moved[ORB * i : ORB * (i + 1), LANES * j : LANES * (j + 1)]
                    if n == m:
                        diag[n] = diag[n] - block
                    else:
                        link[at(n, m)] = -block
                rhs[n] = rhs[n] - moved[ORB * i : ORB * (i + 1), LANES * len(near) :]

    def climb():
        for level in reversed(LEVELS):
            for s, l, r in level:
                near = [n for n in (l, r) if n is not None]
                if not near:
                    sol[s] = rhs[s]
                    continue
                steps = jnp.concatenate([link[at(s, n)] for n in near], axis=1)
                values = jnp.concatenate([right_form(sol[n]) for n in near], axis=0)
                sol[s] = rhs[s] - dot(steps, values)

    climb()
    for s in range(SLABS):
        gain = jnp.sum(
            jnp.where(corner, jnp.broadcast_to(gain_ref[s : s + 1, :], (ORB, LANES)), 0.0),
            axis=1,
            keepdims=True,
        )
        diag[s] = sol[s]
        rhs[s] = gain * sol[s]
    for level in LEVELS:
        for s, l, r in level:
            near = [n for n in (l, r) if n is not None]
            step = dot(inv[s], right_form(rhs[s]))
            rhs[s] = step
            if not near:
                continue
            back = jnp.concatenate([link[at(n, s)] for n in near], axis=0)
            moved = dot(back, right_form(step))
            for i, n in enumerate(near):
                rhs[n] = rhs[n] - moved[ORB * i : ORB * (i + 1)]
    climb()
    first = lane_of((ORB, LANES)) < ORB
    for s in range(SLABS):
        x, y = diag[s], sol[s]
        x_turned = pltpu.roll(x, ORB, 1)
        y_turned = pltpu.roll(y, ORB, 1)
        same = x * y
        crossed = x_turned * y
        pair = jnp.where(first, same + pltpu.roll(same, ORB, 1), crossed - x * y_turned)
        square = x * x
        power = square + pltpu.roll(square, ORB, 1)
        inv[s] = pair
        link[s] = power
        base = (s // 3) * (32 * 9) + (s % 3) * 3
        even = link[s, pl.ds(0, 32, stride=2), :]
        odd = link[s, pl.ds(1, 32, stride=2), :]
        out_ref[pl.ds(base, 32, stride=9), :] = inv[s, pl.ds(0, 32, stride=2), :]
        out_ref[pl.ds(base + 1, 32, stride=9), :] = inv[s, pl.ds(1, 32, stride=2), :]
        out_ref[pl.ds(base + 2, 32, stride=9), :] = jnp.where(lane_of((32, LANES)) < ORB, even, odd)


def solve_all(p, q, src, shift, gain):
    return pl.pallas_call(
        solve_kernel,
        out_shape=jax.ShapeDtypeStruct((SLABS * 96, LANES), F32),
        in_specs=[pl.BlockSpec(memory_space=pltpu.VMEM)] * 5,
        out_specs=pl.BlockSpec(memory_space=pltpu.VMEM),
        scratch_shapes=[
            pltpu.VMEM((SLABS, ORB, LANES), F32),
            pltpu.VMEM((44, ORB, LANES), F32),
            pltpu.VMEM((SLABS, ORB, LANES), F32),
            pltpu.VMEM((SLABS, ORB, LANES), F32),
            pltpu.VMEM((SLABS, ORB, LANES), F32),
        ],
        compiler_params=pltpu.CompilerParams(vmem_limit_bytes=48 << 20),
        name="solve",
    )(p, q, src, shift, gain)


ENERGIES = 64


def lag_kernel(in_ref, out_ref, gl, gg):
    first = lane_of((ENERGIES, LANES)) < ORB
    for half in range(2):
        gl[half, pl.ds(ENERGIES, 8), :] = jnp.zeros((8, LANES), F32)

    def one(index, unused):
        slab = index // 2
        orbital = index % 2
        sums = []
        for half in range(2):
            for parity in range(2):
                base = (half * 2 + parity) * (32 * 9) + slab * 3
                gl[half, pl.ds(parity, 32, stride=2), :] = in_ref[
                    pl.ds(base + orbital, 32, stride=9), :
                ]
                gg[half, pl.ds(parity, 32, stride=2), :] = in_ref[pl.ds(base + 2, 32, stride=9), :]
            power = gg[half]
            turned = pltpu.roll(power, ORB, 1)
            low = jnp.where(first, power, turned)
            high = jnp.where(first, turned, power)
            gg[half] = jnp.where(orbital == 0, low, high)
            acc = [jnp.zeros((8, LANES), F32) for _ in range(8)]
            for energy in range(ENERGIES):
                weight = jnp.broadcast_to(gg[half, energy : energy + 1, :], (8, LANES))
                for block in range((ENERGIES - energy + 7) // 8):
                    acc[block] = acc[block] + weight * gl[half, pl.ds(energy + 8 * block, 8), :]
            sums.append(jnp.concatenate(acc, axis=0))
        zero_turned = pltpu.roll(sums[0], ORB, 1)
        one_turned = pltpu.roll(sums[1], ORB, 1)
        scale = 1.0 / ENERGIES
        out_ref[pl.ds(index, ENERGIES, stride=6), :] = jnp.where(first, sums[0], one_turned) * scale
        out_ref[pl.ds(ENERGIES * 6 + index, ENERGIES, stride=6), :] = (
            jnp.where(first, zero_turned, sums[1]) * scale
        )
        return unused

    lax.fori_loop(0, 6, one, 0)


def correlate(received):
    return pl.pallas_call(
        lag_kernel,
        out_shape=jax.ShapeDtypeStruct((2 * ENERGIES * 6, LANES), F32),
        in_specs=[pl.BlockSpec(memory_space=pltpu.VMEM)],
        out_specs=pl.BlockSpec(memory_space=pltpu.VMEM),
        scratch_shapes=[
            pltpu.VMEM((2, ENERGIES + 8, LANES), F32),
            pltpu.VMEM((2, ENERGIES, LANES), F32),
        ],
        compiler_params=pltpu.CompilerParams(vmem_limit_bytes=32 << 20),
        name="lags",
    )(received)


def row_layout(parts):
    return jnp.concatenate([parts[:, 0], parts[:, 1]], axis=-1)


def per_device(link_p, link_q, shift, lesser_gain, sources):
    group = lax.axis_index("slab")
    halves = [row_layout(sources[..., :ORB]), row_layout(sources[..., ORB:])]
    packed = jnp.stack([row_layout(link_p), row_layout(link_q)] + halves, axis=0)
    packed = lax.all_gather(packed, "slab", axis=1, tiled=True)
    small = jnp.concatenate([shift, lesser_gain], axis=-1)
    small = lax.all_gather(small, "slab", axis=1, tiled=True)
    mine = lax.dynamic_index_in_dim(small, group % 2, 0, keepdims=False)
    src = lax.dynamic_index_in_dim(packed, 2 + group // 2, 0, keepdims=False)
    gain = jnp.concatenate([mine[:, ORB:], mine[:, :ORB]], axis=-1)
    sent = solve_all(packed[0], packed[1], src, mine, gain)
    sent = sent.reshape(4 * 32, 9, LANES)
    received = lax.all_to_all(sent, ("slab", "energy"), split_axis=0, concat_axis=0, tiled=True)
    out = correlate(received.reshape(SLABS * 96, LANES))
    return out.reshape(2, ENERGIES, 3, 2, LANES)


def solution(mesh):
    placed = (
        P("slab", None, None, None),
        P("slab", None, None, None),
        P("energy", "slab", None),
        P("energy", "slab", None),
        P("slab", None, None, None),
    )
    return jax.shard_map(
        per_device,
        mesh=mesh,
        in_specs=placed,
        out_specs=P(None, None, "slab", "energy", None),
        check_vma=False,
    )
```

time: 631 us -> 115 us (0.18); the launches traced: 623 us -> 115 us
  other arithmetic: 394 us -> 1.17 us
  blocking collectives: 90.1 us -> 37.9 us
  matrix products: 43 us -> 0 us
  starting transfers between devices: 41.5 us -> 0.01 us
  Pallas kernels: 0 us -> 38.4 us
  local copies, waits for them, and re-layouts: 30.7 us -> 4.65 us
  between operations: 2.43 us -> 13.5 us
    another operation x48 -> x3, other arithmetic: 391 us -> 1.01 us  [per_device(): jnp.stack([row_layout(link_p), row_layout(link_q)] + halves, axis=0)]
    all_gather x9 -> x1, blocking collectives: 90.1 us -> 10.3 us  [per_device(): small = lax.all_gather(small, 'slab', axis=1, tiled=True)]
    all_to_all x3 -> x0, starting transfers between devices: 41.5 us -> none  [the longest x1 33.5 us: per_device(): lax.all_to_all(elem_power, 'energy', split_axis=2, concat_axis=1, tiled=T...]
    pallas_call x0 -> x2, Pallas kernels: none -> 38.4 us  [the longest x1 35.6 us: solve_all(): pl.pallas_call(solve_kernel, out_shape=jax.ShapeDtypeStruct((SLABS * 96,...]
    all_to_all x0 -> x1, blocking collectives: none -> 27.6 us  [per_device(): lax.all_to_all(sent, ('slab', 'energy'), split_axis=0, concat_axis=0, til...]
    dot_general x59 -> x0, matrix products: 25.4 us -> none  [the longest x28 12.3 us: left_transposed(): return jnp.einsum('...ji,...jk->...ik', left, right, precision=HIGHEST)]
    all_to_all x3 -> x0, waiting for transfers between devices: 20.9 us -> none  [the longest x1 7.41 us: per_device(): lax.all_to_all(elem_im, 'energy', split_axis=2, concat_axis=1, tiled=True)]
    all_gather x0 -> x1, waiting for transfers between devices: none -> 19.2 us  [per_device(): packed = lax.all_gather(packed, 'slab', axis=1, tiled=True)]
  transfers between devices with their start and end apart: 3 -> 1, of which waited for: 3 -> 1; matrix products, arithmetic and copies ran while one was open for 1% -> 0% of each run, Pallas kernels for 0% -> 0%
where the time goes in v1:
time: 115 us
  Pallas kernels  38.4 us (33%)
  blocking collectives  37.9 us (33%)
  waiting for transfers between devices  19.3 us (17%)
  between operations  13.5 us (12%)
  local copies, waits for them, and re-layouts  4.65 us (4%)
  other arithmetic  1.17 us (1%)
    pallas_call x1, Pallas kernels, solve_all(): pl.pallas_call(solve_kernel, out_shape=jax.ShapeDtypeStruct((SLABS * 96,...  35.6 us
    all_to_all x1, blocking collectives, per_device(): lax.all_to_all(sent, ('slab', 'energy'), split_axis=0, concat_axis=0, til...  27.6 us
    all_gather x1, waiting for transfers between devices, per_device(): packed = lax.all_gather(packed, 'slab', axis=1, tiled=True)  19.2 us
    all_gather x1, blocking collectives, per_device(): small = lax.all_gather(small, 'slab', axis=1, tiled=True)  10.3 us
    squeeze x3, local copies, waits for them, and re-layouts, row_layout(): return jnp.concatenate([parts[:, 0], parts[:, 1]], axis=-1)  3.07 us
    pallas_call x1, Pallas kernels, correlate(): pl.pallas_call(lag_kernel, out_shape=jax.ShapeDtypeStruct((2 * ENERGIES *...  2.8 us
  transfers between devices with their start and end apart: 1, of which 1 were waited for; matrix products, arithmetic and copies ran while one was open for 0% of the time, Pallas kernels for 0%

profile of v1, /device:TPU:1, one launch (start us, length us, event | category | flops | bytes accessed | tf_op | source)
XLA Modules:
  0.0 114.8 jit_solution(7752514486452529743)
XLA Ops:
  6.5 0.0 all-gather.2.cloned.1.call-start
  6.5 1.1 slice_bitcast_fusion.5
  7.7 0.0 copy-start
  7.7 0.0 copy-start.1
  7.7 1.0 slice_bitcast_fusion.7
  8.7 1.0 slice_bitcast_fusion.9
  9.6 0.1 maximum_bitcast_fusion.2
  9.8 0.1 maximum_bitcast_fusion
  9.9 0.8 pad_maximum_fusion
  10.7 0.0 all-gather.2.cloned.1.call-update
  10.7 0.0 copy-done
  10.7 0.0 copy-done.1
  10.7 0.1 pad_maximum_fusion.2
  10.8 10.3 %all_gather.7 = f32[2,12,128]{2,0,1:T(2,128)S(1)} all-gather(f32[2,3,128]{2,0,1:T(2,128)S(1)} %pad_maximum_fusion.2), channel_id=1, replica_groups=mesh['slab'=4,'energy'=32] {'slab'}, dimensions={1}, use_global_device_ids=true | all-gather | bytes 15360 | tf_op jit(solution)/shard_map/all_gather | solution.py:334
  21.1 0.1 fusion
  21.2 0.1 pad_maximum_fusion.1.gain_ref
  21.3 19.2 %all-gather.2.cloned.1.call-done = f32[4,12,64,128]{3,2,1,0:T(8,128)} async-done(((f32[4,3,64,128]{3,2,1,0:T(8,128)}), f32[4,12,64,128]{3,2,1,0:T(8,128)}) %all-gather.2.cloned.1.call-update) | async-done | bytes 1572880 | tf_op jit(solution)/shard_map/all_gather | solution.py:332
  40.5 1.3 %dynamic-slice_bitcast_fusion = (f32[12,64,128]{2,1,0:T(8,128)S(1)}, f32[12,64,128]{2,1,0:T(8,128)S(1)}, f32[12,64,128]{2,1,0:T(8,128)S(1)}) fusion(f32[4,12,64,128]{3,2,1,0:T(8,128)} %all-gather.2.cloned.1.call-done, s32[]{:T(128)S(6)} %select_n.20), kind=kLoop, calls=%fused_computation.3 | loop fusion | bytes 2359300 | tf_op jit(solution)/shard_map/jit(dynamic_index_in_dim)/squeeze | solution.py:336
  41.9 35.6 %solve.1 = f32[1152,128]{1,0:T(8,128)S(1)} custom-call(f32[12,64,128]{2,1,0:T(8,128)S(1)} %get-tuple-element.7.p_ref, f32[12,64,128]{2,1,0:T(8,128)S(1)} %get-tuple-element.6.q_ref, f32[12,64,128]{2,1,0:T(8,128)S(1)} %get-tuple-element.5.src_ref, f32[12,128]{1,0:T(8,128)S(1)} %bitcast.51, f32[12,128]{1,0:T(8,128)S(1)} %pad_maximum_fusion.1.gain_ref), custom_call_target="tpu_custom_call" | custom-call | tf_op jit(solution)/shard_map/solve/pallas_call | solution.py:250
  77.5 0.1 reshape.9
  77.5 27.6 %all_to_all.5 = f32[128,9,128]{2,1,0:T(8,128)S(1)} all-to-all(f32[128,9,128]{2,1,0:T(8,128)S(1)} %reshape.9), channel_id=1, replica_groups=mesh['slab'=4,'energy'=32] {'slab','energy'}, dimensions={0} | all-to-all | bytes 1179648 | tf_op jit(solution)/shard_map/all_to_all | solution.py:340
  105.1 0.1 reshape.10.in_ref
  105.2 2.8 %lags.1 = f32[768,128]{1,0:T(8,128)} custom-call(f32[1152,128]{1,0:T(8,128)S(1)} %reshape.10.in_ref), custom_call_target="tpu_custom_call" | custom-call | tf_op jit(solution)/shard_map/lags/pallas_call | solution.py:310
  (2 shorter events, 0.0 us)
Async XLA Ops:
  6.5 34.0 %all-gather.2.cloned.1.call-start = ((), (), s32[]{:S(2)}) async-start(), calls=%async_computation.1 | async-start | bytes 1966080 | tf_op jit(solution)/shard_map/all_gather | solution.py:332
  7.7 3.0 %copy-start = (f32[2,3,64]{2,0,1:T(2,128)S(1)}, f32[2,3,64]{2,0,1:T(2,128)}, u32[]{:S(2)}) copy-start(f32[2,3,64]{2,0,1:T(2,128)} %param.8) | copy-start | bytes 4612
  7.7 3.0 %copy-start.1 = (f32[2,3,64]{2,0,1:T(2,128)S(1)}, f32[2,3,64]{2,0,1:T(2,128)}, u32[]{:S(2)}) copy-start(f32[2,3,64]{2,0,1:T(2,128)} %param.7) | copy-start | bytes 4612
Sparse Core Ops, SparseCore 0:
  10.8 29.6 all-gather.1

commit v2 on v1

--- a/solution.py
+++ b/solution.py
@@ -141,15 +141,18 @@
     return values
 
 
-def solve_kernel(p_ref, q_ref, src_ref, shift_ref, gain_ref, out_ref, diag, link, inv, rhs, sol):
+def solve_kernel(in_ref, small_ref, out_ref, diag, link, inv, rhs, sol):
     slot = {}
 
     def at(i, j):
         return slot.setdefault((i, j), len(slot))
 
     corner = lane_of((ORB, LANES)) == row_of((ORB, LANES))
+    far_corner = lane_of((ORB, LANES)) == row_of((ORB, LANES)) + ORB
     for s in range(SLABS):
-        p, q = p_ref[s], q_ref[s]
+        group, i = divmod(s, 3)
+        p = in_ref[group, 0, i * ORB : (i + 1) * ORB, :]
+        q = in_ref[group, 1, i * ORB : (i + 1) * ORB, :]
         left = jnp.concatenate([p, q], axis=0)
         right = jnp.concatenate([p, times_i(p), q, times_i(q)], axis=0)
         both = lax.dot_general(
@@ -157,7 +160,7 @@
         )
         own = both[ORB:, LANES:]
         before = both[:ORB, :LANES]
-        shift = jnp.broadcast_to(shift_ref[s : s + 1, :], (ORB, LANES))
+        shift = jnp.broadcast_to(small_ref[group, i : i + 1, :], (ORB, LANES))
         own = own + jnp.where(corner, shift, 0.0)
         if s == 0:
             diag[s] = own + before
@@ -166,7 +169,11 @@
             diag[s - 1] = diag[s - 1] + before
             link[at(s - 1, s)] = -both[:ORB, LANES:]
             link[at(s, s - 1)] = -both[ORB:, :LANES]
-        rhs[s] = src_ref[s]
+        for part in range(2):
+            side, offset = divmod(i * ORB + part * 32, HALF_ROWS)
+            rhs[s, part * 32 : part * 32 + 32, :] = in_ref[
+                group, side, LINK_ROWS + offset : LINK_ROWS + offset + 32, :
+            ]
 
     plan = []
     for level in LEVELS:
@@ -208,7 +215,11 @@
     climb()
     for s in range(SLABS):
         gain = jnp.sum(
-            jnp.where(corner, jnp.broadcast_to(gain_ref[s : s + 1, :], (ORB, LANES)), 0.0),
+            jnp.where(
+                far_corner,
+                jnp.broadcast_to(small_ref[s // 3, s % 3 : s % 3 + 1, :], (ORB, LANES)),
+                0.0,
+            ),
             axis=1,
             keepdims=True,
         )
@@ -246,11 +257,11 @@
         out_ref[pl.ds(base + 2, 32, stride=9), :] = jnp.where(lane_of((32, LANES)) < ORB, even, odd)
 
 
-def solve_all(p, q, src, shift, gain):
+def solve_all(gathered, small):
     return pl.pallas_call(
         solve_kernel,
         out_shape=jax.ShapeDtypeStruct((SLABS * 96, LANES), F32),
-        in_specs=[pl.BlockSpec(memory_space=pltpu.VMEM)] * 5,
+        in_specs=[pl.BlockSpec(memory_space=pltpu.VMEM)] * 2,
         out_specs=pl.BlockSpec(memory_space=pltpu.VMEM),
         scratch_shapes=[
             pltpu.VMEM((SLABS, ORB, LANES), F32),
@@ -261,7 +272,7 @@
         ],
         compiler_params=pltpu.CompilerParams(vmem_limit_bytes=48 << 20),
         name="solve",
-    )(p, q, src, shift, gain)
+    )(gathered, small)
 
 
 ENERGIES = 64
@@ -321,23 +332,202 @@
     )(received)
 
 
-def row_layout(parts):
-    return jnp.concatenate([parts[:, 0], parts[:, 1]], axis=-1)
+GROUPS = 4
+PER_GROUP = 32
+LINK_ROWS = 3 * ORB
+HALF_ROWS = LINK_ROWS // 2
+PIECE_ROWS = LINK_ROWS + HALF_ROWS
+CHUNKS = ((0, LINK_ROWS), (LINK_ROWS, HALF_ROWS))
+MESH = pl.DeviceIdType.MESH
+
+
+def gather_kernel(
+    p_ref, q_ref, shift_ref, gain_ref, src_ref, out_ref, small_ref,
+    piece, small_piece, sent, arrived, passed, handed, small_sent, small_arrived,
+):
+    group = lax.axis_index("slab")
+    spot = lax.axis_index("energy")
+    core = lax.rem(spot, 2)
+    sibling = spot + 1 - 2 * core
+    barrier = pltpu.get_barrier_semaphore()
+    for d in range(1, GROUPS):
+        pl.semaphore_signal(
+            barrier, inc=1, device_id=(lax.rem(group + d, GROUPS), spot), device_id_type=MESH
+        )
+    pl.semaphore_signal(barrier, inc=1, device_id=(group, sibling), device_id_type=MESH)
+    my_half = group // 2
+
+    def rows_of(part):
+        return jnp.concatenate([part[0], part[1]], axis=1)
+
+    for i in range(3):
+        p, q = rows_of(p_ref[i]), rows_of(q_ref[i])
+        span = pl.ds(i * ORB, ORB)
+        out_ref[group, 0, span, :] = p
+        out_ref[group, 1, span, :] = q
+        mine = jnp.where(core == 0, p, q)
+        piece[0, span, :] = mine
+        piece[1, span, :] = mine
+        real, imag = src_ref[i, 0], src_ref[i, 1]
+        first = lane_of((ORB, LANES)) < ORB
+        halves = (
+            jnp.where(first, real, pltpu.roll(imag, ORB, 1)),
+            jnp.where(first, pltpu.roll(real, ORB, 1), imag),
+        )
+        own = jnp.where(my_half == 0, halves[0], halves[1])
+        for part in range(2):
+            low = i * ORB + part * 32
+            side, offset = divmod(low, HALF_ROWS)
+            there = pl.ds(LINK_ROWS + offset, 32)
+            rows = slice(part * 32, part * 32 + 32)
+            out_ref[group, side, there, :] = own[rows]
+
+            @pl.when(core == side)
+            def _():
+                piece[0, there, :] = halves[0][rows]
+                piece[1, there, :] = halves[1][rows]
+
+    pair = jnp.concatenate([shift_ref[...], gain_ref[...]], axis=-1)
+    for parity in range(2):
+        small_piece[parity, 0:3, :] = pair[parity]
+    small_ref[group, 0:3, :] = jnp.where(lax.rem(group, 2) == 0, pair[0], pair[1])
+
+    pl.semaphore_wait(barrier, GROUPS)
+    copies = []
+    smalls = []
+    for d in (2, 1, 3):
+        there = lax.rem(group + d, GROUPS)
+        small = pltpu.make_async_remote_copy(
+            src_ref=small_piece.at[lax.rem(there, 2)],
+            dst_ref=small_ref.at[group],
+            send_sem=small_sent.at[d],
+            recv_sem=small_arrived.at[d],
+            device_id=(there, spot),
+            device_id_type=MESH,
+        )
+        small.start()
+        smalls.append(small)
+    for c, (low, rows) in enumerate(CHUNKS):
+        for d in (2, 1, 3):
+            there = lax.rem(group + d, GROUPS)
+            copy = pltpu.make_async_remote_copy(
+                src_ref=piece.at[there // 2, pl.ds(low, rows)],
+                dst_ref=out_ref.at[group, core, pl.ds(low, rows)],
+                send_sem=sent.at[c, d],
+                recv_sem=arrived.at[c, d],
+                device_id=(there, spot),
+                device_id_type=MESH,
+            )
+            copy.start()
+            copies.append((c, low, rows, d, copy))
+    forwards = []
+    for c, low, rows, d, copy in sorted(copies, key=lambda item: (item[0], (1, 3, 2).index(item[3]))):
+        copy.wait_recv()
+        source = lax.rem(group + GROUPS - d, GROUPS)
+        forward = pltpu.make_async_remote_copy(
+            src_ref=out_ref.at[source, core, pl.ds(low, rows)],
+            dst_ref=out_ref.at[source, core, pl.ds(low, rows)],
+            send_sem=passed.at[c, d],
+            recv_sem=handed.at[c, d],
+            device_id=(group, sibling),
+            device_id_type=MESH,
+        )
+        forward.start()
+        forwards.append(forward)
+    for small in smalls:
+        small.wait()
+    for c, low, rows, d, copy in copies:
+        copy.wait_send()
+    for forward in forwards:
+        forward.wait()
+
+
+def gather_links(link_p, link_q, shift, gain, sources):
+    dma = pltpu.SemaphoreType.DMA
+    return pl.pallas_call(
+        gather_kernel,
+        out_shape=(
+            jax.ShapeDtypeStruct((GROUPS, 2, PIECE_ROWS, LANES), F32),
+            jax.ShapeDtypeStruct((GROUPS, 8, LANES), F32),
+        ),
+        in_specs=[pl.BlockSpec(memory_space=pltpu.VMEM)] * 5,
+        out_specs=[pl.BlockSpec(memory_space=pltpu.VMEM)] * 2,
+        scratch_shapes=[
+            pltpu.VMEM((2, PIECE_ROWS, LANES), F32),
+            pltpu.VMEM((2, 8, LANES), F32),
+            dma((2, GROUPS)),
+            dma((2, GROUPS)),
+            dma((2, GROUPS)),
+            dma((2, GROUPS)),
+            dma((GROUPS,)),
+            dma((GROUPS,)),
+        ],
+        compiler_params=pltpu.CompilerParams(
+            collective_id=0, has_side_effects=True, vmem_limit_bytes=16 << 20
+        ),
+        name="gather_links",
+    )(link_p, link_q, shift, gain, sources)
+
+
+def exchange_kernel(in_ref, out_ref, sent, arrived, local):
+    group = lax.axis_index("slab")
+    spot = lax.axis_index("energy")
+    here = group * PER_GROUP + spot
+    count = GROUPS * PER_GROUP
+    barrier = pltpu.get_barrier_semaphore()
+
+    def greet(d, unused):
+        there = lax.rem(here + d, count)
+        pl.semaphore_signal(
+            barrier,
+            inc=1,
+            device_id=(there // PER_GROUP, lax.rem(there, PER_GROUP)),
+            device_id_type=MESH,
+        )
+        return unused
+
+    lax.fori_loop(1, count, greet, 0)
+    own = pltpu.make_async_copy(in_ref.at[here], out_ref.at[here], local)
+    own.start()
+    pl.semaphore_wait(barrier, count - 1)
+
+    def send(d, unused):
+        there = lax.rem(here + d, count)
+        pltpu.make_async_remote_copy(
+            src_ref=in_ref.at[there],
+            dst_ref=out_ref.at[here],
+            send_sem=sent,
+            recv_sem=arrived,
+            device_id=(there // PER_GROUP, lax.rem(there, PER_GROUP)),
+            device_id_type=MESH,
+        ).start()
+        return unused
+
+    lax.fori_loop(1, count, send, 0)
+    own.wait()
+    others = pl.ds(0, count - 1)
+    pltpu.make_async_copy(in_ref.at[others], in_ref.at[others], sent).wait()
+    pltpu.make_async_copy(out_ref.at[others], out_ref.at[others], arrived).wait()
+
+
+def exchange(blocks):
+    return pl.pallas_call(
+        exchange_kernel,
+        out_shape=jax.ShapeDtypeStruct(blocks.shape, F32),
+        in_specs=[pl.BlockSpec(memory_space=pltpu.VMEM)],
+        out_specs=pl.BlockSpec(memory_space=pltpu.VMEM),
+        scratch_shapes=[pltpu.SemaphoreType.DMA, pltpu.SemaphoreType.DMA, pltpu.SemaphoreType.DMA],
+        compiler_params=pltpu.CompilerParams(
+            collective_id=1, has_side_effects=True, vmem_limit_bytes=16 << 20
+        ),
+        name="exchange",
+    )(blocks)
 
 
 def per_device(link_p, link_q, shift, lesser_gain, sources):
-    group = lax.axis_index("slab")
-    halves = [row_layout(sources[..., :ORB]), row_layout(sources[..., ORB:])]
-    packed = jnp.stack([row_layout(link_p), row_layout(link_q)] + halves, axis=0)
-    packed = lax.all_gather(packed, "slab", axis=1, tiled=True)
-    small = jnp.concatenate([shift, lesser_gain], axis=-1)
-    small = lax.all_gather(small, "slab", axis=1, tiled=True)
-    mine = lax.dynamic_index_in_dim(small, group % 2, 0, keepdims=False)
-    src = lax.dynamic_index_in_dim(packed, 2 + group // 2, 0, keepdims=False)
-    gain = jnp.concatenate([mine[:, ORB:], mine[:, :ORB]], axis=-1)
-    sent = solve_all(packed[0], packed[1], src, mine, gain)
-    sent = sent.reshape(4 * 32, 9, LANES)
-    received = lax.all_to_all(sent, ("slab", "energy"), split_axis=0, concat_axis=0, tiled=True)
+    gathered, small = gather_links(link_p, link_q, shift, lesser_gain, sources)
+    sent = solve_all(gathered, small)
+    received = exchange(sent.reshape(GROUPS * PER_GROUP, 9, 1, LANES))
     out = correlate(received.reshape(SLABS * 96, LANES))
     return out.reshape(2, ENERGIES, 3, 2, LANES)
 

time: 115 us -> 75.8 us (0.66)
  blocking collectives: 37.9 us -> 0 us
  Pallas kernels: 38.4 us -> 71.4 us
  waiting for transfers between devices: 19.3 us -> 0 us
  between operations: 13.5 us -> 0.02 us
  other arithmetic: 1.17 us -> 0 us
    pallas_call x0 -> x2, Pallas kernels: none -> 33 us  [the longest x1 19.1 us: exchange(): pl.pallas_call(exchange_kernel, out_shape=jax.ShapeDtypeStruct(blocks.sha...]
    all_to_all x1 -> x0, blocking collectives: 27.6 us -> none  [per_device(): lax.all_to_all(sent, ('slab', 'energy'), split_axis=0, concat_axis=0, til...]
    all_gather x1 -> x0, waiting for transfers between devices: 19.2 us -> none  [per_device(): packed = lax.all_gather(packed, 'slab', axis=1, tiled=True)]
    all_gather x1 -> x0, blocking collectives: 10.3 us -> none  [per_device(): small = lax.all_gather(small, 'slab', axis=1, tiled=True)]
    squeeze x4 -> x0, local copies, waits for them, and re-layouts: 4.42 us -> none  [the longest x3 3.07 us: row_layout(): return jnp.concatenate([parts[:, 0], parts[:, 1]], axis=-1)]
    unnamed x5 -> x8, local copies, waits for them, and re-layouts: 0.02 us -> 4.15 us
  transfers between devices with their start and end apart: 1 -> 0, of which waited for: 1 -> 0; matrix products, arithmetic and copies ran while one was open for 0% -> 0% of each run, Pallas kernels for 0% -> 0%
where the time goes in v2:
time: 75.8 us; the launch traced here: 75.5 us
  Pallas kernels  71.4 us (94%)
  local copies, waits for them, and re-layouts  4.15 us (5%)
    pallas_call x1, Pallas kernels, solve_all(): pl.pallas_call(solve_kernel, out_shape=jax.ShapeDtypeStruct((SLABS * 96,...  35.6 us
    pallas_call x1, Pallas kernels, exchange(): pl.pallas_call(exchange_kernel, out_shape=jax.ShapeDtypeStruct(blocks.sha...  19.1 us
    pallas_call x1, Pallas kernels, gather_links(): pl.pallas_call(gather_kernel, out_shape=(jax.ShapeDtypeStruct((GROUPS, 2,...  13.9 us
    unnamed x8, local copies, waits for them, and re-layouts  4.15 us
    pallas_call x1, Pallas kernels, correlate(): pl.pallas_call(lag_kernel, out_shape=jax.ShapeDtypeStruct((2 * ENERGIES *...  2.8 us

profile of v2, /device:TPU:1, one launch (start us, length us, event | category | flops | bytes accessed | tf_op | source)
XLA Modules:
  0.0 75.5 jit_solution(15961924534540464052)
XLA Ops:
  0.0 0.7 copy.6.shift_ref
  0.7 0.7 copy.7.gain_ref
  1.4 0.0 copy-start
  1.4 0.9 %copy-done = f32[3,2,64,64]{3,2,1,0:T(8,128)S(1)} copy-done((f32[3,2,64,64]{3,2,1,0:T(8,128)S(1)}, f32[3,2,64,64]{3,2,1,0:T(8,128)}, u32[]{:S(2)}) %copy-start) | copy-done | bytes 98328
  2.3 0.0 copy-start.1
  2.3 0.9 %copy-done.1 = f32[3,2,64,64]{3,2,1,0:T(8,128)S(1)} copy-done((f32[3,2,64,64]{3,2,1,0:T(8,128)S(1)}, f32[3,2,64,64]{3,2,1,0:T(8,128)}, u32[]{:S(2)}) %copy-start.1) | copy-done | bytes 98328
  3.2 0.0 copy-start.2
  3.2 0.9 %copy-done.2 = f32[3,2,64,128]{3,2,1,0:T(8,128)S(1)} copy-done((f32[3,2,64,128]{3,2,1,0:T(8,128)S(1)}, f32[3,2,64,128]{3,2,1,0:T(8,128)}, u32[]{:S(2)}) %copy-start.2) | copy-done | bytes 196632
  4.2 13.9 %gather_links.1 = (f32[4,2,288,128]{3,2,1,0:T(8,128)S(1)}, f32[4,8,128]{2,1,0:T(8,128)S(1)}) custom-call(f32[3,2,64,64]{3,2,1,0:T(8,128)S(1)} %copy-done, f32[3,2,64,64]{3,2,1,0:T(8,128)S(1)} %copy-done.1, f32[2,3,64]{2,1,0:T(4,128)S(1)} %copy.6.shift_ref, f32[2,3,64]{2,1,0:T(4,128)S(1)} %copy.7.gain_ref, f32[3,2,64,128]{3,2,1,0:T(8,128)S(1)} %copy-done.2), custom_call_target="tpu_custom_call" | custom-call | tf_op jit(solution)/shard_map/gather_links/pallas_call | solution.py:447
  18.0 35.6 %solve.1 = f32[1152,128]{1,0:T(8,128)S(1)} custom-call(f32[4,2,288,128]{3,2,1,0:T(8,128)S(1)} %get-tuple-element.7.in_ref, f32[4,8,128]{2,1,0:T(8,128)S(1)} %get-tuple-element.8.small_ref), custom_call_target="tpu_custom_call" | custom-call | tf_op jit(solution)/shard_map/solve/pallas_call | solution.py:261
  53.6 19.1 %exchange.1 = f32[128,9,1,128]{3,2,1,0:T(1,128)S(1)} custom-call(f32[128,9,1,128]{3,2,1,0:T(1,128)S(1)} %bitcast.3), custom_call_target="tpu_custom_call" | custom-call | tf_op jit(solution)/shard_map/exchange/pallas_call | solution.py:514
  72.7 2.8 %lags.1 = f32[768,128]{1,0:T(8,128)} custom-call(f32[1152,128]{1,0:T(8,128)S(1)} %bitcast.4), custom_call_target="tpu_custom_call" | custom-call | tf_op jit(solution)/shard_map/lags/pallas_call | solution.py:321
Async XLA Ops:
  1.4 0.9 %copy-start = (f32[3,2,64,64]{3,2,1,0:T(8,128)S(1)}, f32[3,2,64,64]{3,2,1,0:T(8,128)}, u32[]{:S(2)}) copy-start(f32[3,2,64,64]{3,2,1,0:T(8,128)} %p_ref.1) | copy-start | bytes 294916
  2.3 0.9 %copy-start.1 = (f32[3,2,64,64]{3,2,1,0:T(8,128)S(1)}, f32[3,2,64,64]{3,2,1,0:T(8,128)}, u32[]{:S(2)}) copy-start(f32[3,2,64,64]{3,2,1,0:T(8,128)} %q_ref.1) | copy-start | bytes 294916
  3.2 0.9 %copy-start.2 = (f32[3,2,64,128]{3,2,1,0:T(8,128)S(1)}, f32[3,2,64,128]{3,2,1,0:T(8,128)}, u32[]{:S(2)}) copy-start(f32[3,2,64,128]{3,2,1,0:T(8,128)} %src_ref.1) | copy-start | bytes 589828

commit v3 on v2

v3 whole, which is shorter than its diff:
```python
import functools

import jax
import jax.numpy as jnp
from jax import lax
from jax.experimental import pallas as pl
from jax.experimental.pallas import tpu as pltpu
from jax.sharding import PartitionSpec as P

HIGHEST = lax.Precision.HIGHEST
F32 = jnp.float32
ORB = 64
LANES = 128
SLABS = 12
LEVELS = (
    ((0, None, 1), (2, 1, 3), (4, 3, 5), (6, 5, 7), (8, 7, 9), (10, 9, 11)),
    ((1, None, 3), (5, 3, 7), (9, 7, 11)),
    ((3, None, 7), (11, 7, None)),
    ((7, None, None),),
)
STEPS = {6: 1, 3: 2, 2: 2, 1: 2}


def lane_of(shape):
    return lax.broadcasted_iota(jnp.int32, shape, len(shape) - 1)


def row_of(shape):
    return lax.broadcasted_iota(jnp.int32, shape, len(shape) - 2)


def times_i(value):
    turned = pltpu.roll(value, ORB, 1)
    return jnp.where(lane_of(value.shape) < ORB, -turned, turned)


def right_form(value):
    return jnp.concatenate([value, times_i(value)], axis=0)


def dot(left, right):
    return jnp.dot(left, right, precision=HIGHEST, preferred_element_type=F32)


def spread(row):
    return jnp.broadcast_to(row, (8, LANES))


def pack(values):
    first = lane_of((8, LANES)) < ORB
    pairs = []
    for at in range(0, len(values), 2):
        one = values[at]
        two = values[min(at + 1, len(values) - 1)]
        real, imag = [], []
        for t in range(0, ORB, 8):
            x, y = one[t : t + 8], two[t : t + 8]
            real.append(jnp.where(first, x, pltpu.roll(y, ORB, 1)))
            imag.append(jnp.where(first, pltpu.roll(x, ORB, 1), y))
        pairs.append((real, imag))
    return pairs


def unpack(pairs, count):
    first = lane_of((8, LANES)) < ORB
    values = []
    for real, imag in pairs:
        left = [jnp.where(first, r, pltpu.roll(i, ORB, 1)) for r, i in zip(real, imag)]
        values.append(jnp.concatenate(left, axis=0))
        if len(values) < count:
            right = [jnp.where(first, pltpu.roll(r, ORB, 1), i) for r, i in zip(real, imag)]
            values.append(jnp.concatenate(right, axis=0))
    return values


def pivot_inverse(gram, size):
    if size == 1:
        return [[(1.0 / gram[0, 0][0], None)]]
    one, two = gram[0, 0][0], gram[1, 1][0]
    re, im = gram[0, 1]
    scale = 1.0 / (one * two - re * re - im * im)
    re, im = re * scale, im * scale
    return [[(two * scale, None), (-re, -im)], [(-re, im), (one * scale, None)]]


def invert_all(values, size):
    lanes = lane_of((8, LANES))
    place = lanes & (ORB - 1)
    half = lanes & ORB
    rows = row_of((8, LANES))

    def column(tile, k):
        return jnp.take_along_axis(tile, half + k, axis=1, mode="promise_in_bounds")

    def pivot_block(real, imag, k):
        tile, row = divmod(k, 8)
        gram = {}
        for j in range(size):
            re, im = column(real[tile], k + j), column(imag[tile], k + j)
            for i in range(j + 1):
                at = slice(row + i, row + i + 1)
                gram[i, j] = (spread(re[at]), None if i == j else spread(im[at]))
        return gram

    state = [
        (real, imag, pivot_inverse(pivot_block(real, imag, 0), size))
        for real, imag in pack(values)
    ]
    for k in range(0, ORB, size):
        tile, row = divmod(k, 8)
        later = []
        for real, imag, small in state:
            cols = [
                ([column(x, k + j) for x in real], [column(x, k + j) for x in imag])
                for j in range(size)
            ]
            ahead = None
            if k + size < ORB:
                gram = pivot_block(real, imag, k + size)
                next_tile, next_row = divmod(k + size, 8)
                near = []
                for re, im in cols:
                    near.append([])
                    for i in range(size):
                        at = slice(next_row + i, next_row + i + 1)
                        near[-1].append((spread(re[next_tile][at]), spread(im[next_tile][at])))
                for j in range(size):
                    for m in range(size):
                        re = im = None
                        for q in range(size):
                            gr, gi = small[m][q]
                            cr, ci = near[q][j]
                            tr, ti = gr * cr, -(gr * ci)
                            if gi is not None:
                                tr, ti = tr + gi * ci, ti + gi * cr
                            re, im = (tr, ti) if re is None else (re + tr, im + ti)
                        for i in range(j + 1):
                            cr, ci = near[m][i]
                            old_re, old_im = gram[i, j]
                            new_re = old_re - (cr * re - ci * im)
                            new_im = None if i == j else old_im - (cr * im + ci * re)
                            gram[i, j] = (new_re, new_im)
                ahead = pivot_inverse(gram, size)
            tops = []
            for j in range(size):
                at = slice(row + j, row + j + 1)
                tops.append((spread(real[tile][at]), spread(imag[tile][at])))
            fresh = []
            for i in range(size):
                re = im = None
                for j in range(size):
                    gr, gi = small[i][j]
                    tr, ti = gr * tops[j][0], gr * tops[j][1]
                    if gi is not None:
                        tr, ti = tr - gi * tops[j][1], ti + gi * tops[j][0]
                    re, im = (tr, ti) if re is None else (re + tr, im + ti)
                for j in range(size):
                    gr, gi = small[i][j]
                    re = jnp.where(place == k + j, gr, re)
                    im = jnp.where(place == k + j, 0.0 if gi is None else gi, im)
                fresh.append((re, im))
            inside = (place >= k) & (place < k + size)
            new_real, new_imag = [], []
            for t in range(ORB // 8):
                re = jnp.where(inside, 0.0, real[t])
                im = jnp.where(inside, 0.0, imag[t])
                for j in range(size):
                    cr, ci = cols[j][0][t], cols[j][1][t]
                    re = re - cr * fresh[j][0] + ci * fresh[j][1]
                    im = im - cr * fresh[j][1] - ci * fresh[j][0]
                if t == tile:
                    for j in range(size):
                        re = jnp.where(rows == row + j, fresh[j][0], re)
                        im = jnp.where(rows == row + j, fresh[j][1], im)
                new_real.append(re)
                new_imag.append(im)
            later.append((new_real, new_imag, ahead))
        state = later
    return unpack([(real, imag) for real, imag, unused in state], len(values))


def link_slots():
    slots = {}
    for level in LEVELS:
        for s, l, r in level:
            near = [n for n in (l, r) if n is not None]
            for n in near:
                for m in near:
                    if m != n:
                        slots.setdefault((n, m), len(slots))
                slots.setdefault((s, n), len(slots))
                slots.setdefault((n, s), len(slots))
    return slots


SLOTS = link_slots()
INV, SOL, LINK = 0, SLABS, 2 * SLABS
KEPT = 2 * SLABS + len(SLOTS)


def climb(kept, rhs, sol):
    def link(i, j):
        return kept[LINK + SLOTS[i, j]]

    for level in reversed(LEVELS):
        for s, l, r in level:
            near = [n for n in (l, r) if n is not None]
            if not near:
                sol(s, rhs[s])
                continue
            steps = jnp.concatenate([link(s, n) for n in near], axis=1)
            values = jnp.concatenate([right_form(sol(n)) for n in near], axis=0)
            sol(s, rhs[s] - dot(steps, values))


def solve_kernel(in_ref, small_ref, kept, diag, rhs):
    def link(i, j):
        return LINK + SLOTS[i, j]

    corner = lane_of((ORB, LANES)) == row_of((ORB, LANES))
    for s in range(SLABS):
        group, i = divmod(s, 3)
        p = in_ref[group, 0, i * ORB : (i + 1) * ORB, :]
        q = in_ref[group, 1, i * ORB : (i + 1) * ORB, :]
        left = jnp.concatenate([p, q], axis=0)
        right = jnp.concatenate([p, times_i(p), q, times_i(q)], axis=0)
        both = lax.dot_general(
            left, right, (((1,), (1,)), ((), ())), precision=HIGHEST, preferred_element_type=F32
        )
        own = both[ORB:, LANES:]
        before = both[:ORB, :LANES]
        shift = jnp.broadcast_to(small_ref[group, i : i + 1, :], (ORB, LANES))
        own = own + jnp.where(corner, shift, 0.0)
        if s == 0:
            diag[s] = own + before
        else:
            diag[s] = own
            diag[s - 1] = diag[s - 1] + before
            kept[link(s - 1, s)] = -both[:ORB, LANES:]
            kept[link(s, s - 1)] = -both[ORB:, :LANES]
        for part in range(2):
            side, offset = divmod(i * ORB + part * 32, HALF_ROWS)
            rhs[s, part * 32 : part * 32 + 32, :] = in_ref[
                group, side, LINK_ROWS + offset : LINK_ROWS + offset + 32, :
            ]

    for level in LEVELS:
        inverses = invert_all([diag[s] for s, _, _ in level], STEPS[len(level)])
        for (s, l, r), inverse in zip(level, inverses):
            kept[INV + s] = inverse
        for s, l, r in level:
            near = [n for n in (l, r) if n is not None]
            sides = [right_form(kept[link(s, n)]) for n in near] + [right_form(rhs[s])]
            step = dot(kept[INV + s], jnp.concatenate(sides, axis=1))
            rhs[s] = step[:, LANES * len(near) :]
            if not near:
                continue
            back = jnp.concatenate([kept[link(n, s)] for n in near], axis=0)
            pieces = [step[:, LANES * i : LANES * (i + 1)] for i in range(len(near) + 1)]
            moved = dot(back, jnp.concatenate([right_form(piece) for piece in pieces], axis=1))
            for i, n in enumerate(near):
                kept[link(s, n)] = pieces[i]
                for j, m in enumerate(near):
                    block = moved[ORB * i : ORB * (i + 1), LANES * j : LANES * (j + 1)]
                    if n == m:
                        diag[n] = diag[n] - block
                    else:
                        kept[link(n, m)] = -block
                rhs[n] = rhs[n] - moved[ORB * i : ORB * (i + 1), LANES * len(near) :]

    def sol(s, value=None):
        if value is None:
            return kept[SOL + s]
        kept[SOL + s] = value

    climb(kept, rhs, sol)


def solve_retarded(gathered, small):
    return pl.pallas_call(
        solve_kernel,
        out_shape=jax.ShapeDtypeStruct((KEPT, ORB, LANES), F32),
        in_specs=[pl.BlockSpec(memory_space=pltpu.VMEM)] * 2,
        out_specs=pl.BlockSpec(memory_space=pltpu.VMEM),
        scratch_shapes=[
            pltpu.VMEM((SLABS, ORB, LANES), F32),
            pltpu.VMEM((SLABS, ORB, LANES), F32),
        ],
        compiler_params=pltpu.CompilerParams(vmem_limit_bytes=32 << 20),
        name="retarded",
    )(gathered, small)


ENERGIES = 64


def lag_kernel(in_ref, out_ref, gl, gg):
    first = lane_of((ENERGIES, LANES)) < ORB
    for half in range(2):
        gl[half, pl.ds(ENERGIES, 8), :] = jnp.zeros((8, LANES), F32)

    def one(index, unused):
        slab = index // 2
        orbital = index % 2
        sums = []
        for half in range(2):
            for parity in range(2):
                base = (half * 2 + parity) * (32 * 9) + slab * 3
                gl[half, pl.ds(parity, 32, stride=2), :] = in_ref[
                    pl.ds(base + orbital, 32, stride=9), :
                ]
                gg[half, pl.ds(parity, 32, stride=2), :] = in_ref[pl.ds(base + 2, 32, stride=9), :]
            power = gg[half]
            turned = pltpu.roll(power, ORB, 1)
            low = jnp.where(first, power, turned)
            high = jnp.where(first, turned, power)
            gg[half] = jnp.where(orbital == 0, low, high)
            acc = [jnp.zeros((8, LANES), F32) for _ in range(8)]
            for energy in range(ENERGIES):
                weight = jnp.broadcast_to(gg[half, energy : energy + 1, :], (8, LANES))
                for block in range((ENERGIES - energy + 7) // 8):
                    acc[block] = acc[block] + weight * gl[half, pl.ds(energy + 8 * block, 8), :]
            sums.append(jnp.concatenate(acc, axis=0))
        zero_turned = pltpu.roll(sums[0], ORB, 1)
        one_turned = pltpu.roll(sums[1], ORB, 1)
        scale = 1.0 / ENERGIES
        out_ref[pl.ds(index, ENERGIES, stride=6), :] = jnp.where(first, sums[0], one_turned) * scale
        out_ref[pl.ds(ENERGIES * 6 + index, ENERGIES, stride=6), :] = (
            jnp.where(first, zero_turned, sums[1]) * scale
        )
        return unused

    lax.fori_loop(0, 6, one, 0)


def correlate(received):
    return pl.pallas_call(
        lag_kernel,
        out_shape=jax.ShapeDtypeStruct((2 * ENERGIES * 6, LANES), F32),
        in_specs=[pl.BlockSpec(memory_space=pltpu.VMEM)],
        out_specs=pl.BlockSpec(memory_space=pltpu.VMEM),
        scratch_shapes=[
            pltpu.VMEM((2, ENERGIES + 8, LANES), F32),
            pltpu.VMEM((2, ENERGIES, LANES), F32),
        ],
        compiler_params=pltpu.CompilerParams(vmem_limit_bytes=32 << 20),
        name="lags",
    )(received)


GROUPS = 4
PER_GROUP = 32
LINK_ROWS = 3 * ORB
HALF_ROWS = LINK_ROWS // 2
PIECE_ROWS = LINK_ROWS + HALF_ROWS
CHUNKS = ((0, LINK_ROWS), (LINK_ROWS, HALF_ROWS))
MESH = pl.DeviceIdType.MESH


def gather_kernel(
    packed_ref, pair_ref, out_ref, small_ref,
    piece, small_piece, sent, arrived, passed, handed, small_sent, small_arrived,
):
    group = lax.axis_index("slab")
    spot = lax.axis_index("energy")
    core = lax.rem(spot, 2)
    sibling = spot + 1 - 2 * core
    barrier = pltpu.get_barrier_semaphore()
    for d in range(1, GROUPS):
        pl.semaphore_signal(
            barrier, inc=1, device_id=(lax.rem(group + d, GROUPS), spot), device_id_type=MESH
        )
    pl.semaphore_signal(barrier, inc=1, device_id=(group, sibling), device_id_type=MESH)
    my_half = group // 2

    first = lane_of((ORB, LANES)) < ORB
    for i in range(3):
        real, imag = packed_ref[i, 0, :, :LANES], packed_ref[i, 1, :, :LANES]
        p = jnp.where(first, real, pltpu.roll(imag, ORB, 1))
        q = jnp.where(first, pltpu.roll(real, ORB, 1), imag)
        span = pl.ds(i * ORB, ORB)
        out_ref[group, 0, span, :] = p
        out_ref[group, 1, span, :] = q
        mine = jnp.where(core == 0, p, q)
        piece[0, span, :] = mine
        piece[1, span, :] = mine
        real, imag = packed_ref[i, 0, :, LANES:], packed_ref[i, 1, :, LANES:]
        halves = (
            jnp.where(first, real, pltpu.roll(imag, ORB, 1)),
            jnp.where(first, pltpu.roll(real, ORB, 1), imag),
        )
        own = jnp.where(my_half == 0, halves[0], halves[1])
        for part in range(2):
            low = i * ORB + part * 32
            side, offset = divmod(low, HALF_ROWS)
            there = pl.ds(LINK_ROWS + offset, 32)
            rows = slice(part * 32, part * 32 + 32)
            out_ref[group, side, there, :] = own[rows]

            @pl.when(core == side)
            def _():
                piece[0, there, :] = halves[0][rows]
                piece[1, there, :] = halves[1][rows]

    pair = pair_ref[...]
    for parity in range(2):
        small_piece[parity, 0:3, :] = pair[:, parity]
    small_ref[group, 0:3, :] = jnp.where(lax.rem(group, 2) == 0, pair[:, 0], pair[:, 1])

    pl.semaphore_wait(barrier, GROUPS)
    copies = []
    smalls = []
    for d in (2, 1, 3):
        there = lax.rem(group + d, GROUPS)
        small = pltpu.make_async_remote_copy(
            src_ref=small_piece.at[lax.rem(there, 2)],
            dst_ref=small_ref.at[group],
            send_sem=small_sent.at[d],
            recv_sem=small_arrived.at[d],
            device_id=(there, spot),
            device_id_type=MESH,
        )
        small.start()
        smalls.append(small)
    for c, (low, rows) in enumerate(CHUNKS):
        for d in (2, 1, 3):
            there = lax.rem(group + d, GROUPS)
            copy = pltpu.make_async_remote_copy(
                src_ref=piece.at[there // 2, pl.ds(low, rows)],
                dst_ref=out_ref.at[group, core, pl.ds(low, rows)],
                send_sem=sent.at[c, d],
                recv_sem=arrived.at[c, d],
                device_id=(there, spot),
                device_id_type=MESH,
            )
            copy.start()
            copies.append((c, low, rows, d, copy))
    forwards = []
    for c, low, rows, d, copy in sorted(copies, key=lambda item: (item[0], (1, 3, 2).index(item[3]))):
        copy.wait_recv()
        source = lax.rem(group + GROUPS - d, GROUPS)
        forward = pltpu.make_async_remote_copy(
            src_ref=out_ref.at[source, core, pl.ds(low, rows)],
            dst_ref=out_ref.at[source, core, pl.ds(low, rows)],
            send_sem=passed.at[c, d],
            recv_sem=handed.at[c, d],
            device_id=(group, sibling),
            device_id_type=MESH,
        )
        forward.start()
        forwards.append(forward)
    for small in smalls:
        small.wait()
    for c, low, rows, d, copy in copies:
        copy.wait_send()
    for forward in forwards:
        forward.wait()


def gather_links(packed, pair):
    dma = pltpu.SemaphoreType.DMA
    return pl.pallas_call(
        gather_kernel,
        out_shape=(
            jax.ShapeDtypeStruct((GROUPS, 2, PIECE_ROWS, LANES), F32),
            jax.ShapeDtypeStruct((GROUPS, 8, LANES), F32),
        ),
        in_specs=[pl.BlockSpec(memory_space=pltpu.VMEM)] * 2,
        out_specs=[pl.BlockSpec(memory_space=pltpu.VMEM)] * 2,
        scratch_shapes=[
            pltpu.VMEM((2, PIECE_ROWS, LANES), F32),
            pltpu.VMEM((2, 8, LANES), F32),
            dma((2, GROUPS)),
            dma((2, GROUPS)),
            dma((2, GROUPS)),
            dma((2, GROUPS)),
            dma((GROUPS,)),
            dma((GROUPS,)),
        ],
        compiler_params=pltpu.CompilerParams(
            collective_id=0, has_side_effects=True, vmem_limit_bytes=16 << 20
        ),
        name="gather_links",
    )(packed, pair)


def exchange_kernel(kept, small_ref, out_ref, rhs, sol_ref, scratch, outgoing, sent, arrived, local):
    group = lax.axis_index("slab")
    spot = lax.axis_index("energy")
    here = group * PER_GROUP + spot
    count = GROUPS * PER_GROUP
    barrier = pltpu.get_barrier_semaphore()

    def greet(d, unused):
        there = lax.rem(here + d, count)
        pl.semaphore_signal(
            barrier,
            inc=1,
            device_id=(there // PER_GROUP, lax.rem(there, PER_GROUP)),
            device_id_type=MESH,
        )
        return unused

    lax.fori_loop(1, count, greet, 0)

    corner = lane_of((ORB, LANES)) == row_of((ORB, LANES)) + ORB
    for s in range(SLABS):
        row = jnp.broadcast_to(small_ref[s // 3, s % 3 : s % 3 + 1, :], (ORB, LANES))
        gain = jnp.sum(jnp.where(corner, row, 0.0), axis=1, keepdims=True)
        rhs[s] = gain * kept[SOL + s]
    for level in LEVELS:
        for s, l, r in level:
            near = [n for n in (l, r) if n is not None]
            step = dot(kept[INV + s], right_form(rhs[s]))
            rhs[s] = step
            if not near:
                continue
            back = jnp.concatenate([kept[LINK + SLOTS[n, s]] for n in near], axis=0)
            moved = dot(back, right_form(step))
            for i, n in enumerate(near):
                rhs[n] = rhs[n] - moved[ORB * i : ORB * (i + 1)]

    def sol(s, value=None):
        if value is None:
            return sol_ref[s]
        sol_ref[s] = value

    climb(kept, rhs, sol)
    first = lane_of((ORB, LANES)) < ORB
    for s in range(SLABS):
        x, y = kept[SOL + s], sol_ref[s]
        same = x * y
        crossed = pltpu.roll(x, ORB, 1) * y
        turned = x * pltpu.roll(y, ORB, 1)
        square = x * x
        scratch[0, s] = jnp.where(first, same + pltpu.roll(same, ORB, 1), crossed - turned)
        scratch[1, s] = square + pltpu.roll(square, ORB, 1)
        there = pl.ds((s // 3) * PER_GROUP, PER_GROUP)
        low = (s % 3) * 3
        even = scratch[1, s, pl.ds(0, 32, stride=2), :]
        odd = scratch[1, s, pl.ds(1, 32, stride=2), :]
        outgoing[there, low, 0, :] = scratch[0, s, pl.ds(0, 32, stride=2), :]
        outgoing[there, low + 1, 0, :] = scratch[0, s, pl.ds(1, 32, stride=2), :]
        outgoing[there, low + 2, 0, :] = jnp.where(lane_of((32, LANES)) < ORB, even, odd)

    own = pltpu.make_async_copy(outgoing.at[here], out_ref.at[here], local)
    own.start()
    pl.semaphore_wait(barrier, count - 1)

    def send(d, unused):
        there = lax.rem(here + d, count)
        pltpu.make_async_remote_copy(
            src_ref=outgoing.at[there],
            dst_ref=out_ref.at[here],
            send_sem=sent,
            recv_sem=arrived,
            device_id=(there // PER_GROUP, lax.rem(there, PER_GROUP)),
            device_id_type=MESH,
        ).start()
        return unused

    lax.fori_loop(1, count, send, 0)
    own.wait()
    others = pl.ds(0, count - 1)
    pltpu.make_async_copy(outgoing.at[others], outgoing.at[others], sent).wait()
    pltpu.make_async_copy(out_ref.at[others], out_ref.at[others], arrived).wait()


def lesser_and_exchange(kept, small):
    block = (GROUPS * PER_GROUP, 9, 1, LANES)
    return pl.pallas_call(
        exchange_kernel,
        out_shape=jax.ShapeDtypeStruct(block, F32),
        in_specs=[pl.BlockSpec(memory_space=pltpu.VMEM)] * 2,
        out_specs=pl.BlockSpec(memory_space=pltpu.VMEM),
        scratch_shapes=[
            pltpu.VMEM((SLABS, ORB, LANES), F32),
            pltpu.VMEM((SLABS, ORB, LANES), F32),
            pltpu.VMEM((2, SLABS, ORB, LANES), F32),
            pltpu.VMEM(block, F32),
            pltpu.SemaphoreType.DMA,
            pltpu.SemaphoreType.DMA,
            pltpu.SemaphoreType.DMA,
        ],
        compiler_params=pltpu.CompilerParams(
            collective_id=1, has_side_effects=True, vmem_limit_bytes=24 << 20
        ),
        name="lesser_and_exchange",
    )(kept, small)


def per_device(link_p, link_q, shift, lesser_gain, sources):
    packed = jnp.concatenate([link_p, link_q, sources], axis=-1)
    pair = jnp.swapaxes(jnp.concatenate([shift, lesser_gain], axis=-1), 0, 1)
    gathered, small = gather_links(packed, pair)
    kept = solve_retarded(gathered, small)
    received = lesser_and_exchange(kept, small)
    out = correlate(received.reshape(SLABS * 96, LANES))
    return out.reshape(2, ENERGIES, 3, 2, LANES)


def solution(mesh):
    placed = (
        P("slab", None, None, None),
        P("slab", None, None, None),
        P("energy", "slab", None),
        P("energy", "slab", None),
        P("slab", None, None, None),
    )
    return jax.shard_map(
        per_device,
        mesh=mesh,
        in_specs=placed,
        out_specs=P(None, None, "slab", "energy", None),
        check_vma=False,
    )
```

time: 75.8 us -> 60.6 us (0.80)
  Pallas kernels: 71.4 us -> 58.4 us
  local copies, waits for them, and re-layouts: 4.15 us -> 0 us
  other arithmetic: 0 us -> 2.06 us
    pallas_call x2, Pallas kernels: 54.7 us -> 41.6 us  [the longest x1 21.1 us: solve_retarded(): pl.pallas_call(solve_kernel, out_shape=jax.ShapeDtypeStruct((KEPT, ORB, L...]
    unnamed x8 -> x0, local copies, waits for them, and re-layouts: 4.15 us -> none
    concatenate x0 -> x1, other arithmetic: none -> 1.28 us  [per_device(): packed = jnp.concatenate([link_p, link_q, sources], axis=-1)]
    transpose x0 -> x1, other arithmetic: none -> 0.77 us  [per_device(): pair = jnp.swapaxes(jnp.concatenate([shift, lesser_gain], axis=-1), 0, 1)]
where the time goes in v3:
time: 60.6 us; the launch traced here: 60.5 us
  Pallas kernels  58.4 us (96%)
  other arithmetic  2.06 us (3%)
    pallas_call x1, Pallas kernels, solve_retarded(): pl.pallas_call(solve_kernel, out_shape=jax.ShapeDtypeStruct((KEPT, ORB, L...  21.1 us
    pallas_call x1, Pallas kernels, lesser_and_exchange(): pl.pallas_call(exchange_kernel, out_shape=jax.ShapeDtypeStruct(block, F32...  20.5 us
    pallas_call x1, Pallas kernels, gather_links(): pl.pallas_call(gather_kernel, out_shape=(jax.ShapeDtypeStruct((GROUPS, 2,...  14 us
    pallas_call x1, Pallas kernels, correlate(): pl.pallas_call(lag_kernel, out_shape=jax.ShapeDtypeStruct((2 * ENERGIES *...  2.8 us
    concatenate x1, other arithmetic, per_device(): packed = jnp.concatenate([link_p, link_q, sources], axis=-1)  1.28 us

profile of v3, /device:TPU:1, one launch (start us, length us, event | category | flops | bytes accessed | tf_op | source)
XLA Modules:
  0.0 60.5 jit_solution(13348275670349042827)
XLA Ops:
  0.0 0.8 %maximum_bitcast_fusion.pair_ref = f32[3,2,128]{2,1,0:T(2,128)S(1)} fusion(f32[2,3,64]{2,0,1:T(2,128)} %param.8, f32[2,3,64]{2,0,1:T(2,128)} %param.7), kind=kLoop, calls=%fused_computation.1 | loop fusion | flops 768 | bytes 6144 | tf_op jit(solution)/shard_map/transpose | solution.py:594
  0.8 1.3 %pad_maximum_fusion.packed_ref = f32[3,2,64,256]{3,2,1,0:T(8,128)S(1)} fusion(f32[3,2,64,128]{3,2,1,0:T(8,128)} %param.9, f32[3,2,64,64]{3,2,1,0:T(8,128)} %param.6, f32[3,2,64,64]{3,2,1,0:T(8,128)} %param.5), kind=kLoop, calls=%fused_computation | loop fusion | flops 196608 | bytes 786432 | tf_op jit(solution)/shard_map/concatenate | solution.py:593
  2.1 14.0 %gather_links.1 = (f32[4,2,288,128]{3,2,1,0:T(8,128)S(1)}, f32[4,8,128]{2,1,0:T(8,128)S(1)}) custom-call(f32[3,2,64,256]{3,2,1,0:T(8,128)S(1)} %pad_maximum_fusion.packed_ref, f32[3,2,128]{2,1,0:T(2,128)S(1)} %maximum_bitcast_fusion.pair_ref), custom_call_target="tpu_custom_call" | custom-call | tf_op jit(solution)/shard_map/gather_links/pallas_call | solution.py:462
  16.0 21.1 %retarded.1.kept = f32[60,64,128]{2,1,0:T(8,128)S(1)} custom-call(f32[4,2,288,128]{3,2,1,0:T(8,128)S(1)} %get-tuple-element.7.in_ref, f32[4,8,128]{2,1,0:T(8,128)S(1)} %get-tuple-element.8.small_ref), custom_call_target="tpu_custom_call" | custom-call | tf_op jit(solution)/shard_map/retarded/pallas_call | solution.py:280
  37.2 20.5 %lesser_and_exchange.1 = f32[128,9,1,128]{3,2,1,0:T(1,128)S(1)} custom-call(f32[60,64,128]{2,1,0:T(8,128)S(1)} %retarded.1.kept, f32[4,8,128]{2,1,0:T(8,128)S(1)} %get-tuple-element.8.small_ref), custom_call_target="tpu_custom_call" | custom-call | tf_op jit(solution)/shard_map/lesser_and_exchange/pallas_call | solution.py:571
  57.7 2.8 %lags.1 = f32[768,128]{1,0:T(8,128)} custom-call(f32[1152,128]{1,0:T(8,128)S(1)} %bitcast.4), custom_call_target="tpu_custom_call" | custom-call | tf_op jit(solution)/shard_map/lags/pallas_call | solution.py:337

commit v4 on v3

--- a/solution.py
+++ b/solution.py
@@ -353,7 +353,6 @@
 LINK_ROWS = 3 * ORB
 HALF_ROWS = LINK_ROWS // 2
 PIECE_ROWS = LINK_ROWS + HALF_ROWS
-CHUNKS = ((0, LINK_ROWS), (LINK_ROWS, HALF_ROWS))
 MESH = pl.DeviceIdType.MESH
 
 
@@ -408,7 +407,6 @@
     small_ref[group, 0:3, :] = jnp.where(lax.rem(group, 2) == 0, pair[:, 0], pair[:, 1])
 
     pl.semaphore_wait(barrier, GROUPS)
-    copies = []
     smalls = []
     for d in (2, 1, 3):
         there = lax.rem(group + d, GROUPS)
@@ -422,28 +420,38 @@
         )
         small.start()
         smalls.append(small)
-    for c, (low, rows) in enumerate(CHUNKS):
-        for d in (2, 1, 3):
-            there = lax.rem(group + d, GROUPS)
-            copy = pltpu.make_async_remote_copy(
-                src_ref=piece.at[there // 2, pl.ds(low, rows)],
-                dst_ref=out_ref.at[group, core, pl.ds(low, rows)],
-                send_sem=sent.at[c, d],
-                recv_sem=arrived.at[c, d],
-                device_id=(there, spot),
-                device_id_type=MESH,
-            )
-            copy.start()
-            copies.append((c, low, rows, d, copy))
+    def rows_at(chunk):
+        return pl.ds(chunk * HALF_ROWS, HALF_ROWS)
+
+    def to_group(chunk, d, there, source_ref, origin):
+        return pltpu.make_async_remote_copy(
+            src_ref=source_ref,
+            dst_ref=out_ref.at[origin, core, rows_at(chunk)],
+            send_sem=sent.at[chunk, d],
+            recv_sem=arrived.at[chunk, d],
+            device_id=(there, spot),
+            device_id_type=MESH,
+        )
+
+    copies = {}
+    for chunk, d in ((0, 1), (1, 3), (1, 1), (0, 3), (2, 2), (2, 1), (2, 3)):
+        there = lax.rem(group + d, GROUPS)
+        half = there // 2 if chunk == 2 else 0
+        copies[chunk, d] = to_group(chunk, d, there, piece.at[half, rows_at(chunk)], group)
+        copies[chunk, d].start()
     forwards = []
-    for c, low, rows, d, copy in sorted(copies, key=lambda item: (item[0], (1, 3, 2).index(item[3]))):
-        copy.wait_recv()
-        source = lax.rem(group + GROUPS - d, GROUPS)
+    for chunk, d in ((0, 1), (1, 3), (1, 1), (0, 3), (2, 1), (2, 3), (0, 2), (1, 2), (2, 2)):
+        origin = lax.rem(group + GROUPS - d, GROUPS)
+        copies[chunk, d].wait_recv()
+        here = out_ref.at[origin, core, rows_at(chunk)]
+        if (chunk, d) in ((0, 1), (1, 3)):
+            copies[chunk, 2] = to_group(chunk, 2, lax.rem(group + d, GROUPS), here, origin)
+            copies[chunk, 2].start()
         forward = pltpu.make_async_remote_copy(
-            src_ref=out_ref.at[source, core, pl.ds(low, rows)],
-            dst_ref=out_ref.at[source, core, pl.ds(low, rows)],
-            send_sem=passed.at[c, d],
-            recv_sem=handed.at[c, d],
+            src_ref=here,
+            dst_ref=here,
+            send_sem=passed.at[chunk, d],
+            recv_sem=handed.at[chunk, d],
             device_id=(group, sibling),
             device_id_type=MESH,
         )
@@ -451,7 +459,7 @@
         forwards.append(forward)
     for small in smalls:
         small.wait()
-    for c, low, rows, d, copy in copies:
+    for copy in copies.values():
         copy.wait_send()
     for forward in forwards:
         forward.wait()
@@ -470,10 +478,10 @@
         scratch_shapes=[
             pltpu.VMEM((2, PIECE_ROWS, LANES), F32),
             pltpu.VMEM((2, 8, LANES), F32),
-            dma((2, GROUPS)),
-            dma((2, GROUPS)),
-            dma((2, GROUPS)),
-            dma((2, GROUPS)),
+            dma((3, GROUPS)),
+            dma((3, GROUPS)),
+            dma((3, GROUPS)),
+            dma((3, GROUPS)),
             dma((GROUPS,)),
             dma((GROUPS,)),
         ],
@@ -501,7 +509,15 @@
         )
         return unused
 
-    lax.fori_loop(1, count, greet, 0)
+    def greet_eight(i, unused):
+        for j in range(8):
+            greet(1 + 8 * i + j, 0)
+        return unused
+
+    full = (count - 1) // 8
+    lax.fori_loop(0, full, greet_eight, 0)
+    for d in range(1 + 8 * full, count):
+        greet(d, 0)
 
     corner = lane_of((ORB, LANES)) == row_of((ORB, LANES)) + ORB
     for s in range(SLABS):
@@ -547,8 +563,7 @@
     own.start()
     pl.semaphore_wait(barrier, count - 1)
 
-    def send(d, unused):
-        there = lax.rem(here + d, count)
+    def send(there):
         pltpu.make_async_remote_copy(
             src_ref=outgoing.at[there],
             dst_ref=out_ref.at[here],
@@ -557,9 +572,24 @@
             device_id=(there // PER_GROUP, lax.rem(there, PER_GROUP)),
             device_id_type=MESH,
         ).start()
-        return unused
-
-    lax.fori_loop(1, count, send, 0)
+
+    z, x, core = spot // 8, lax.rem(spot // 2, 4), lax.rem(spot, 2)
+    hops = (0, 1, 2, 1)
+    planes = [(dy, dz) for dy in range(4) for dz in range(4)]
+    planes.sort(key=lambda plane: -(hops[plane[0]] + hops[plane[1]]))
+    for dy, dz in planes:
+        plane = lax.rem(group + dy, 4) * PER_GROUP + lax.rem(z + dz, 4) * 8
+
+        def spread_x(i, unused):
+            dx = lax.rem(i // 2 + 2, 4)
+            send(plane + lax.rem(x + dx, 4) * 2 + lax.rem(core + i, 2))
+            return unused
+
+        if (dy, dz) == (0, 0):
+            for i in (0, 1, 2, 3, 6, 7, 5):
+                spread_x(jnp.int32(i), 0)
+        else:
+            lax.fori_loop(0, 8, spread_x, 0, unroll=True)
     own.wait()
     others = pl.ds(0, count - 1)
     pltpu.make_async_copy(outgoing.at[others], outgoing.at[others], sent).wait()

time: 60.6 us -> 58.5 us (0.965)
  Pallas kernels: 58.4 us -> 56.3 us
    pallas_call x1, Pallas kernels: 20.5 us -> 19.3 us  [lesser_and_exchange(): pl.pallas_call(exchange_kernel, out_shape=jax.ShapeDtypeStruct(block, F32...]
    pallas_call x1, Pallas kernels: 14 us -> 13.1 us  [gather_links(): pl.pallas_call(gather_kernel, out_shape=(jax.ShapeDtypeStruct((GROUPS, 2,...]
where the time goes in v4:
time: 58.5 us; the launch traced here: 58.4 us
  Pallas kernels  56.3 us (96%)
  other arithmetic  2.06 us (4%)
    pallas_call x1, Pallas kernels, solve_retarded(): pl.pallas_call(solve_kernel, out_shape=jax.ShapeDtypeStruct((KEPT, ORB, L...  21.1 us
    pallas_call x1, Pallas kernels, lesser_and_exchange(): pl.pallas_call(exchange_kernel, out_shape=jax.ShapeDtypeStruct(block, F32...  19.3 us
    pallas_call x1, Pallas kernels, gather_links(): pl.pallas_call(gather_kernel, out_shape=(jax.ShapeDtypeStruct((GROUPS, 2,...  13.1 us
    pallas_call x1, Pallas kernels, correlate(): pl.pallas_call(lag_kernel, out_shape=jax.ShapeDtypeStruct((2 * ENERGIES *...  2.8 us
    concatenate x1, other arithmetic, per_device(): packed = jnp.concatenate([link_p, link_q, sources], axis=-1)  1.28 us

profile of v4, /device:TPU:1, one launch (start us, length us, event | category | flops | bytes accessed | tf_op | source)
XLA Modules:
  0.0 58.4 jit_solution(17818888028993904297)
XLA Ops:
  0.0 0.8 %maximum_bitcast_fusion.pair_ref = f32[3,2,128]{2,1,0:T(2,128)S(1)} fusion(f32[2,3,64]{2,0,1:T(2,128)} %param.8, f32[2,3,64]{2,0,1:T(2,128)} %param.7), kind=kLoop, calls=%fused_computation.1 | loop fusion | flops 768 | bytes 6144 | tf_op jit(solution)/shard_map/transpose | solution.py:624
  0.8 1.3 %pad_maximum_fusion.packed_ref = f32[3,2,64,256]{3,2,1,0:T(8,128)S(1)} fusion(f32[3,2,64,128]{3,2,1,0:T(8,128)} %param.9, f32[3,2,64,64]{3,2,1,0:T(8,128)} %param.6, f32[3,2,64,64]{3,2,1,0:T(8,128)} %param.5), kind=kLoop, calls=%fused_computation | loop fusion | flops 196608 | bytes 786432 | tf_op jit(solution)/shard_map/concatenate | solution.py:623
  2.1 13.1 %gather_links.1 = (f32[4,2,288,128]{3,2,1,0:T(8,128)S(1)}, f32[4,8,128]{2,1,0:T(8,128)S(1)}) custom-call(f32[3,2,64,256]{3,2,1,0:T(8,128)S(1)} %pad_maximum_fusion.packed_ref, f32[3,2,128]{2,1,0:T(2,128)S(1)} %maximum_bitcast_fusion.pair_ref), custom_call_target="tpu_custom_call" | custom-call | tf_op jit(solution)/shard_map/gather_links/pallas_call | solution.py:470
  15.1 21.1 %retarded.1.kept = f32[60,64,128]{2,1,0:T(8,128)S(1)} custom-call(f32[4,2,288,128]{3,2,1,0:T(8,128)S(1)} %get-tuple-element.7.in_ref, f32[4,8,128]{2,1,0:T(8,128)S(1)} %get-tuple-element.8.small_ref), custom_call_target="tpu_custom_call" | custom-call | tf_op jit(solution)/shard_map/retarded/pallas_call | solution.py:280
  36.2 19.3 %lesser_and_exchange.1 = f32[128,9,1,128]{3,2,1,0:T(1,128)S(1)} custom-call(f32[60,64,128]{2,1,0:T(8,128)S(1)} %retarded.1.kept, f32[4,8,128]{2,1,0:T(8,128)S(1)} %get-tuple-element.8.small_ref), custom_call_target="tpu_custom_call" | custom-call | tf_op jit(solution)/shard_map/lesser_and_exchange/pallas_call | solution.py:601
  55.6 2.8 %lags.1 = f32[768,128]{1,0:T(8,128)} custom-call(f32[1152,128]{1,0:T(8,128)S(1)} %bitcast.4), custom_call_target="tpu_custom_call" | custom-call | tf_op jit(solution)/shard_map/lags/pallas_call | solution.py:337

commit v5 on v4

--- a/solution.py
+++ b/solution.py
@@ -330,7 +330,7 @@
         )
         return unused
 
-    lax.fori_loop(0, 6, one, 0)
+    lax.fori_loop(0, 6, one, 0, unroll=True)
 
 
 def correlate(received):

time: 58.5 us -> 58.3 us (level)
  no operation moved by 1% of the time
where the time goes in v5:
time: 58.3 us; the launch traced here: 58.2 us
  Pallas kernels  56.1 us (96%)
  other arithmetic  2.06 us (4%)
    pallas_call x1, Pallas kernels, solve_retarded(): pl.pallas_call(solve_kernel, out_shape=jax.ShapeDtypeStruct((KEPT, ORB, L...  21.1 us
    pallas_call x1, Pallas kernels, lesser_and_exchange(): pl.pallas_call(exchange_kernel, out_shape=jax.ShapeDtypeStruct(block, F32...  19.6 us
    pallas_call x1, Pallas kernels, gather_links(): pl.pallas_call(gather_kernel, out_shape=(jax.ShapeDtypeStruct((GROUPS, 2,...  13.1 us
    pallas_call x1, Pallas kernels, correlate(): pl.pallas_call(lag_kernel, out_shape=jax.ShapeDtypeStruct((2 * ENERGIES *...  2.36 us
    concatenate x1, other arithmetic, per_device(): packed = jnp.concatenate([link_p, link_q, sources], axis=-1)  1.28 us

profile of v5, /device:TPU:1, one launch (start us, length us, event | category | flops | bytes accessed | tf_op | source)
XLA Modules:
  0.0 58.2 jit_solution(14078682096841207981)
XLA Ops:
  0.0 0.8 %maximum_bitcast_fusion.pair_ref = f32[3,2,128]{2,1,0:T(2,128)S(1)} fusion(f32[2,3,64]{2,0,1:T(2,128)} %param.8, f32[2,3,64]{2,0,1:T(2,128)} %param.7), kind=kLoop, calls=%fused_computation.1 | loop fusion | flops 768 | bytes 6144 | tf_op jit(solution)/shard_map/transpose | solution.py:624
  0.8 1.3 %pad_maximum_fusion.packed_ref = f32[3,2,64,256]{3,2,1,0:T(8,128)S(1)} fusion(f32[3,2,64,128]{3,2,1,0:T(8,128)} %param.9, f32[3,2,64,64]{3,2,1,0:T(8,128)} %param.6, f32[3,2,64,64]{3,2,1,0:T(8,128)} %param.5), kind=kLoop, calls=%fused_computation | loop fusion | flops 196608 | bytes 786432 | tf_op jit(solution)/shard_map/concatenate | solution.py:623
  2.1 13.1 %gather_links.1 = (f32[4,2,288,128]{3,2,1,0:T(8,128)S(1)}, f32[4,8,128]{2,1,0:T(8,128)S(1)}) custom-call(f32[3,2,64,256]{3,2,1,0:T(8,128)S(1)} %pad_maximum_fusion.packed_ref, f32[3,2,128]{2,1,0:T(2,128)S(1)} %maximum_bitcast_fusion.pair_ref), custom_call_target="tpu_custom_call" | custom-call | tf_op jit(solution)/shard_map/gather_links/pallas_call | solution.py:470
  15.1 21.1 %retarded.1.kept = f32[60,64,128]{2,1,0:T(8,128)S(1)} custom-call(f32[4,2,288,128]{3,2,1,0:T(8,128)S(1)} %get-tuple-element.7.in_ref, f32[4,8,128]{2,1,0:T(8,128)S(1)} %get-tuple-element.8.small_ref), custom_call_target="tpu_custom_call" | custom-call | tf_op jit(solution)/shard_map/retarded/pallas_call | solution.py:280
  36.2 19.6 %lesser_and_exchange.1 = f32[128,9,1,128]{3,2,1,0:T(1,128)S(1)} custom-call(f32[60,64,128]{2,1,0:T(8,128)S(1)} %retarded.1.kept, f32[4,8,128]{2,1,0:T(8,128)S(1)} %get-tuple-element.8.small_ref), custom_call_target="tpu_custom_call" | custom-call | tf_op jit(solution)/shard_map/lesser_and_exchange/pallas_call | solution.py:601
  55.8 2.4 %lags.1 = f32[768,128]{1,0:T(8,128)} custom-call(f32[1152,128]{1,0:T(8,128)S(1)} %bitcast.4), custom_call_target="tpu_custom_call" | custom-call | tf_op jit(solution)/shard_map/lags/pallas_call | solution.py:337
